TPU v7x, 32 devices: a whole 2x2x4 slice. The times are simulated.
32 devices in a mesh: img: 8 (over z, x), seq: 4 (over y, core).
Axes of the slice: x: 2, y: 2, z: 4, core: 2. Of those that a mesh axis runs over, the one named last changes fastest.
Arguments:
- tokens: bfloat16 [4864, 1024], P(('img', 'seq')), may hold values from -6 to 6
- classes: int32 [32], P('img'), may hold values 0 or 1
- source_index: int32 [145, 4], replicated, may hold values from 0 to 49
- position_table: float32 [50, 1024], replicated, may hold values from -3 to 3
- input_weight: bfloat16 [1024, 3072], P('img'), may hold values from -0.1875 to 0.1875
- query_bias: float32 [1024], replicated, may hold values from -3 to 3
- value_bias: float32 [1024], replicated, may hold values from -3 to 3
- output_weight: bfloat16 [1024, 1024], P('img'), may hold values from -0.75 to 0.75
- output_bias: float32 [1024], replicated, may hold values from -2 to 2
- up_weight: bfloat16 [1024, 4096], P('img'), may hold values from -0.1875 to 0.1875
- up_bias: float32 [4096], replicated, may hold values from -3 to 3
- down_weight: bfloat16 [4096, 1024], P('img'), may hold values from -0.09375 to 0.09375
- down_bias: float32 [1024], replicated, may hold values from -2 to 2
- first_gain: float32 [1024], replicated, may hold values from 0.5 to 1.5
- first_shift: float32 [1024], replicated, may hold values from -2 to 2
- second_gain: float32 [1024], replicated, may hold values from 0.5 to 1.5
- second_shift: float32 [1024], replicated, may hold values from -2 to 2
- cotangent: bfloat16 [4864, 1024], P(('img', 'seq')), may hold values from -6 to 6
Outputs:
- block_out: bfloat16 [4864, 1024], P(('img', 'seq'))
- tokens_grad: bfloat16 [4864, 1024], P(('img', 'seq'))
- position_grad: float32 [50, 1024], replicated
- input_weight_grad: float32 [1024, 3072], P('img')
- query_bias_grad: float32 [1024], replicated
- value_bias_grad: float32 [1024], replicated
- output_weight_grad: float32 [1024, 1024], P('img')
- output_bias_grad: float32 [1024], replicated
- up_weight_grad: float32 [1024, 4096], P('img')
- up_bias_grad: float32 [4096], replicated
- down_weight_grad: float32 [4096, 1024], P('img')
- down_bias_grad: float32 [1024], replicated
- first_gain_grad: float32 [1024], replicated
- first_shift_grad: float32 [1024], replicated
- second_gain_grad: float32 [1024], replicated
- second_shift_grad: float32 [1024], replicated
Inputs may be any that keep to these rules, and one draw needn't show every extreme that they name: `classes`: 0 marks an image of 50 tokens, 1 an image of 145 tokens; the 4 images of one index of img fill its slots end to end in order, the rest being padding.
All inputs are finite; a program needn't handle non-finite values. No bound on the sum of `classes` on one device may be relied on, other than what follows from the above.
Results may differ from a plain program's by a relative error of at most 0.013.
Values may be sent and summed in bfloat16 or wider, within the bound.
No kernel may reach another device: no remote copies, remote signals or barrier semaphores. Data moves between devices by JAX's collectives and lax.ppermute only.
A program may use at most 192 MiB of HBM per device.

v0:
```python
import jax
import jax.numpy as jnp
from jax import lax
from jax.experimental import pallas as pl
from jax.experimental.pallas import tpu as pltpu
from jax.sharding import PartitionSpec as P

HEADS = 16
HEAD_DIM = 64
TABLE = 50
LONG = 145
IMG_GRP = 4


highest = lax.Precision.HIGHEST
epsilon = 1e-06
masked_value = -1e30


def layer_norm(inputs, norm_gain, norm_shift):
    average = jnp.mean(inputs, axis=-1, keepdims=True)
    centred = inputs - average
    spread = jnp.mean(centred * centred, axis=-1, keepdims=True)
    return centred * lax.rsqrt(spread + epsilon) * norm_gain + norm_shift


def exact_gelu(inputs):
    return jax.nn.gelu(inputs, approximate=False)


def slot_segments(classes, slot_ids):
    counts = TABLE + (LONG - TABLE) * classes
    image_ends = jnp.cumsum(counts)
    segment = jnp.sum((slot_ids[:, None] >= image_ends[None, :]).astype(jnp.int32), axis=1)
    return (segment, image_ends - counts)


def table_mixing(classes, slot_ids, source_index):
    segment, starts = slot_segments(classes, slot_ids)
    images = jnp.arange(IMG_GRP, dtype=jnp.int32)
    picked = segment[:, None] == images[None, :]
    valid = segment < IMG_GRP
    start_of = jnp.sum(jnp.where(picked, starts[None, :], 0), axis=1)
    larger = jnp.sum(jnp.where(picked, classes[None, :], 0), axis=1) > 0
    place = jnp.where(valid, slot_ids - start_of, 0)
    columns = jnp.arange(TABLE, dtype=jnp.int32)
    direct = (place[:, None] == columns[None, :]).astype(jnp.float32)
    positions = jnp.arange(LONG, dtype=jnp.int32)
    sources = jnp.sum(
        jnp.where(place[:, None, None] == positions[None, :, None], source_index[None, :, :], 0),
        axis=1,
    )
    across = ((place * 7 % 12).astype(jnp.float32) + 0.5) / 12.0
    downward = ((place * 5 % 12).astype(jnp.float32) + 0.5) / 12.0
    corners = jnp.stack(
        [
            (1.0 - across) * (1.0 - downward),
            (1.0 - across) * downward,
            across * (1.0 - downward),
            across * downward,
        ],
        axis=1,
    )
    blended = jnp.sum(
        jnp.where(sources[:, :, None] == columns[None, None, :], corners[:, :, None], 0.0), axis=1
    )
    mixing = jnp.where(
        (valid & larger)[:, None], blended, jnp.where((valid & ~larger)[:, None], direct, 0.0)
    )
    return (segment, valid, mixing)


GROUP = 4
f32 = jnp.float32
bf16 = jnp.bfloat16


def exchange(value, axis, distance):
    size = lax.axis_size(axis)
    return lax.ppermute(value, axis, [(i, i ^ distance) for i in range(size)])


def phases(size):
    found, stride = [], size
    while stride > 1:
        radix = 4 if stride % 4 == 0 else 2
        stride //= radix
        found.append((stride, radix))
    return found


def gather_relative(shard):
    parts = {0: shard}
    for stride, radix in phases(lax.axis_size("img")):
        held = dict(parts)
        if len(held) <= 4:
            for j, part in held.items():
                for digit in range(1, radix):
                    parts[j ^ (digit * stride)] = exchange(part, "img", digit * stride)
        else:
            order = sorted(held)
            stacked = jnp.stack([held[j] for j in order])
            for digit in range(1, radix):
                received = exchange(stacked, "img", digit * stride)
                for position, j in enumerate(order):
                    parts[j ^ (digit * stride)] = received[position]
    return [parts[j] for j in range(len(parts))]


def scatter_relative(pieces):
    held = {j: piece for j, piece in enumerate(pieces)}
    for stride, radix in reversed(phases(lax.axis_size("img"))):
        keep = sorted(j for j in held if (j // stride) % radix == 0)
        total = {j: held[j] for j in keep}
        order = [j for j in keep if j != 0] + [0]
        if len(keep) <= 4:
            for j in order:
                for digit in range(1, radix):
                    sent = held[j + digit * stride].astype(bf16)
                    total[j] = total[j] + exchange(sent, "img", digit * stride).astype(f32)
        else:
            for digit in range(1, radix):
                sent = jnp.stack([held[j + digit * stride].astype(bf16) for j in keep])
                received = exchange(sent, "img", digit * stride)
                for position, j in enumerate(keep):
                    total[j] = total[j] + received[position].astype(f32)
        held = total
    return held[0]


def group_gather(value):
    across = exchange(value, "seq", 2)
    beside = exchange(value, "seq", 1)
    return [value, beside, across, exchange(across, "seq", 1)]


def group_scatter(parts):
    beside = exchange(jnp.stack([parts[3], parts[1]]).astype(bf16), "seq", 1)
    far = parts[2] + beside[0].astype(f32)
    near = parts[0] + beside[1].astype(f32)
    return near + exchange(far.astype(bf16), "seq", 2).astype(f32)


def place_kernel(count):
    def kernel(index_ref, *refs):
        for j in range(count):
            refs[count][index_ref[j]] = refs[j][...]

    return kernel


def place(parts, mine):
    count = len(parts)
    index = mine ^ jnp.arange(count, dtype=jnp.int32)
    return pl.pallas_call(
        place_kernel(count),
        out_shape=jax.ShapeDtypeStruct((count,) + parts[0].shape, parts[0].dtype),
        in_specs=[pl.BlockSpec(memory_space=pltpu.SMEM)]
        + [pl.BlockSpec(memory_space=pltpu.VMEM)] * count,
        out_specs=pl.BlockSpec(memory_space=pltpu.VMEM),
        name="place",
    )(index, *parts)


def sum_everywhere(value):
    rows = value.shape[0] // 2
    seq = lax.axis_index("seq")
    low, high = seq & 1, (seq >> 1) & 1
    halves = value.reshape(2, rows, -1)
    mine = mine_of(halves, low, 0) + exchange(mine_of(halves, 1 - low, 0), "seq", 1)
    halves = mine.reshape(2, rows // 2, -1)
    mine = mine_of(halves, high, 0) + exchange(mine_of(halves, 1 - high, 0), "seq", 2)
    for stride, radix in reversed(phases(lax.axis_size("img"))):
        others = [mine] + [exchange(mine, "img", digit * stride) for digit in range(1, radix)]
        while len(others) > 1:
            others = [others[i] + others[i + 1] for i in range(0, len(others), 2)]
        mine = others[0]
    other = exchange(mine, "seq", 2)
    mine = jnp.where(high == 0, jnp.concatenate([mine, other]), jnp.concatenate([other, mine]))
    other = exchange(mine, "seq", 1)
    return jnp.where(low == 0, jnp.concatenate([mine, other]), jnp.concatenate([other, mine]))


def reorder(parts, mine):
    stacked = jnp.stack(parts)
    return [lax.dynamic_index_in_dim(stacked, mine ^ p, 0, keepdims=False) for p in range(GROUP)]


def mine_of(array, mine, axis):
    return lax.dynamic_index_in_dim(array, mine, axis, keepdims=False)


VMEM = pl.BlockSpec(memory_space=pltpu.VMEM)
SMEM = pl.BlockSpec(memory_space=pltpu.SMEM)
ROWS = (((0,), (0,)), ((), ()))
LAST = (((1,), (1,)), ((), ()))


def local_call(kernel, outs, inputs, scratch=()):
    return pl.pallas_call(
        kernel,
        out_shape=[jax.ShapeDtypeStruct(shape, kind) for shape, kind in outs],
        in_specs=[SMEM] + [VMEM] * (len(inputs) - 1),
        out_specs=[VMEM] * len(outs),
        scratch_shapes=list(scratch),
        compiler_params=pltpu.CompilerParams(vmem_limit_bytes=56 * 1024 * 1024),
    )(*inputs)


def pick(sources, blocks, outs, index):
    count = len(blocks)

    def kernel(index_ref, *refs):
        ins, results, sems = refs[: len(sources)], refs[len(sources) : -1], refs[-1]
        copies = []
        for number, (source, axis, start, out, there, length) in enumerate(blocks):
            begin = pl.multiple_of(start + index_ref[0] * length, length)
            if axis == 0:
                origin, target = ins[source].at[pl.ds(begin, length), :], results[out]
            else:
                origin = ins[source].at[:, pl.ds(begin, length)]
                target = results[out].at[:, pl.ds(there, length)]
            copies.append(pltpu.make_async_copy(origin, target, sems.at[number]))
        for copy in copies:
            copy.start()
        for copy in copies:
            copy.wait()

    return pl.pallas_call(
        kernel,
        out_shape=[jax.ShapeDtypeStruct(shape, bf16) for shape in outs],
        in_specs=[SMEM] + [pl.BlockSpec(memory_space=pl.ANY)] * len(sources),
        out_specs=[VMEM] * len(outs),
        scratch_shapes=[pltpu.SemaphoreType.DMA((count,))],
    )(index, *sources)


def place_in(index_ref, parts, out, source, target):
    rows = parts[0].shape[0]
    for j, part in enumerate(parts):
        at = pl.ds(pl.multiple_of(index_ref[j] * rows, rows), rows)
        out[at, target[0] : target[1]] = part[:, source[0] : source[1]]


def attention_forward(index, normed, firsts, seconds, query_bias, value_bias, segments):
    slots, width = normed.shape
    part = width // GROUP
    heads = part // HEAD_DIM
    rows = slots // GROUP
    count = len(firsts)
    scale = HEAD_DIM ** (-0.5)

    def kernel(index_ref, x_ref, *refs):
        halves, refs = (refs[:count], refs[count : 2 * count]), refs[2 * count :]
        qb_ref, vb_ref, seg_rows, seg_cols = refs[:4]
        w_out, wo_out, q_out, k_out, v_out, att_out, total_out = refs[4:]
        place_in(index_ref, halves[0], w_out, (0, 2 * part), (0, 2 * part))
        place_in(index_ref, halves[1], w_out, (0, part), (2 * part, 3 * part))
        place_in(index_ref, halves[1], wo_out, (part, 2 * part), (0, part))
        projected = jnp.dot(x_ref[...], w_out[...], preferred_element_type=f32)
        queries = (projected[:, :part] + qb_ref[...]).astype(bf16)
        for block in range(GROUP):
            q_out[block] = queries[block * rows : (block + 1) * rows]
        k_out[...] = projected[:, part : 2 * part].astype(bf16)
        v_out[...] = (projected[:, 2 * part :] + vb_ref[...]).astype(bf16)

        def step(block, carry):
            same = seg_rows[block] == seg_cols[...]
            mixed, totals = [], []
            for h in range(heads):
                lanes = slice(h * HEAD_DIM, (h + 1) * HEAD_DIM)
                raw = lax.dot_general(
                    q_out[block, :, lanes], k_out[:, lanes], LAST, preferred_element_type=f32
                )
                logits = jnp.where(same, raw * scale, masked_value)
                top = jnp.max(logits, axis=-1, keepdims=True)
                raised = jnp.exp(logits - top)
                total = jnp.sum(raised, axis=-1, keepdims=True)
                probs = (raised * (1.0 / total)).astype(bf16)
                mixed.append(jnp.dot(probs, v_out[:, lanes], preferred_element_type=f32))
                totals.append(top + jnp.log(total))
            att_out[block] = jnp.concatenate(mixed, axis=1).astype(bf16)
            total_out[block] = jnp.concatenate(totals, axis=1)
            return carry

        lax.fori_loop(0, GROUP, step, 0)

    outs = [
        ((width, 3 * part), bf16),
        ((width, part), bf16),
        ((GROUP, rows, part), bf16),
        ((slots, part), bf16),
        ((slots, part), bf16),
        ((GROUP, rows, part), bf16),
        ((GROUP, rows, heads), f32),
    ]
    inputs = [index, normed, *firsts, *seconds, query_bias[None], value_bias[None]]
    inputs += [segments.reshape(GROUP, rows, 1), segments[None]]
    return local_call(kernel, outs, inputs)


def attention_backward(queries, keys, values, mixed_grad, totals, segments):
    blocks, rows, part = queries.shape
    slots = keys.shape[0]
    heads = part // HEAD_DIM
    scale = HEAD_DIM ** (-0.5)

    def kernel(zero_ref, q_ref, k_ref, v_ref, g_ref, t_ref, seg_rows, seg_cols, out, sums, acc):
        acc[...] = jnp.zeros_like(acc)

        def step(block, carry):
            same = seg_rows[block] == seg_cols[...]
            q_grads, k_grads, v_grads = [], [], []
            for h in range(heads):
                lanes = slice(h * HEAD_DIM, (h + 1) * HEAD_DIM)
                query, key, grad = q_ref[block, :, lanes], k_ref[:, lanes], g_ref[block, :, lanes]
                raw = lax.dot_general(query, key, LAST, preferred_element_type=f32)
                logits = jnp.where(same, raw * scale, masked_value)
                probs = jnp.exp(logits - t_ref[block, :, h : h + 1])
                probs_grad = lax.dot_general(
                    grad, v_ref[:, lanes], LAST, preferred_element_type=f32
                )
                weighted = probs * probs_grad
                inner = jnp.sum(weighted, axis=-1, keepdims=True)
                score = (scale * (weighted - probs * inner)).astype(bf16)
                q_grads.append(jnp.dot(score, key, preferred_element_type=f32))
                k_grads.append(
                    lax.dot_general(score, query, ROWS, preferred_element_type=f32)
                )
                v_grads.append(
                    lax.dot_general(probs.astype(bf16), grad, ROWS, preferred_element_type=f32)
                )
            start = pl.multiple_of(block * rows, 8)
            acc[pl.ds(start, rows), :part] = jnp.concatenate(q_grads, axis=1)
            acc[:, part:] += jnp.concatenate(k_grads + v_grads, axis=1)
            return carry

        lax.fori_loop(0, blocks, step, 0)
        rounded = acc[...].astype(bf16)
        out[...] = rounded
        sums[...] = jnp.sum(rounded.astype(f32), axis=0, keepdims=True)

    outs = [((slots, 3 * part), bf16), ((1, 3 * part), f32)]
    inputs = [jnp.zeros((1,), jnp.int32), queries, keys, values]
    inputs += [mixed_grad.reshape(blocks, rows, part), totals]
    inputs += [segments.reshape(blocks, rows, 1), segments[None]]
    scratch = [pltpu.VMEM((slots, 3 * part), f32)]
    return local_call(kernel, outs, inputs, scratch)


def feed_forward(index, seconds, parts, bias):
    rows, width = seconds[0].shape
    count, units = len(parts), parts[0].shape[1]
    half = 0.5**0.5

    def kernel(index_ref, *refs):
        xs, refs = refs[:GROUP], refs[GROUP:]
        weights, refs = refs[:count], refs[count:]
        b_ref, w_out, x_out, active_out, slope_out, upper = refs
        place_in(index_ref, weights, w_out, (0, units), (0, units))
        for j in range(GROUP):
            x_out[j] = xs[j][...]
            upper[...] = jnp.dot(xs[j][...], w_out[...], preferred_element_type=f32) + b_ref[...]

            def step(i, carry, j=j):
                at = pl.ds(pl.multiple_of(i * 8, 8), 8)
                u = upper[at, :]
                share = 0.5 * (1.0 + lax.erf(u * half))
                upper[at, :] = u * share
                slope_out[j, at, :] = share + u * jnp.exp(-0.5 * u * u) * 0.3989422804014327
                return carry

            lax.fori_loop(0, rows // 8, step, 0)
            active_out[j] = upper[...].astype(bf16)

    outs = [
        ((width, units), bf16),
        ((GROUP, rows, width), bf16),
        ((GROUP, rows, units), bf16),
        ((GROUP, rows, units), f32),
    ]
    inputs = [index, *seconds, *parts, bias[None]]
    return local_call(kernel, outs, inputs, [pltpu.VMEM((rows, units), f32)])


def feed_backward(index, upstream, parts, slope, up_full):
    blocks, rows, units = slope.shape
    width = upstream.shape[-1]
    count = len(parts)

    def kernel(index_ref, g_ref, *refs):
        weights, refs = refs[:count], refs[count:]
        s_ref, up_ref, w_out, upper_out, sums, sent, kept = refs
        place_in(index_ref, weights, w_out, (0, width), (0, width))
        for j in (3, 1, 2, 0):
            grad = lax.dot_general(g_ref[j], w_out[...], LAST, preferred_element_type=f32)
            low = (grad * s_ref[j]).astype(bf16)
            upper_out[j] = low
            total = jnp.sum(low.astype(f32), axis=0, keepdims=True)
            sums[...] = total if j == 3 else sums[...] + total
            back = lax.dot_general(low, up_ref[...], LAST, preferred_element_type=f32)
            if j % 2:
                sent[(3 - j) // 2] = back.astype(bf16)
            else:
                kept[(2 - j) // 2] = back

    outs = [
        ((count * parts[0].shape[0], width), bf16),
        ((blocks, rows, units), bf16),
        ((1, units), f32),
        ((2, rows, width), bf16),
        ((2, rows, width), f32),
    ]
    return local_call(kernel, outs, [index, upstream, *parts, slope, up_full])


def weight_pieces(index, left, right):
    count = index.shape[0]
    rows = left.shape[1] // count
    shape = (count // 2, rows, right.shape[1])

    def kernel(index_ref, left_ref, right_ref, sent, kept):
        for j in [*range(1, count, 2), *range(0, count, 2)]:
            block = left_ref[:, pl.ds(pl.multiple_of(index_ref[j] * rows, rows), rows)]
            term = lax.dot_general(block, right_ref[...], ROWS, preferred_element_type=f32)
            if j % 2:
                sent[j // 2] = term.astype(bf16)
            else:
                kept[j // 2] = term

    return local_call(kernel, [(shape, bf16), (shape, f32)], [index, left, right])


def group_terms(owners, left, right):
    columns = right.shape[1] // GROUP

    def kernel(owner_ref, left_ref, right_ref, *outs):
        for j in range(GROUP):
            start = pl.multiple_of(owner_ref[j] * columns, columns)
            block = right_ref[:, pl.ds(start, columns)]
            term = lax.dot_general(left_ref[...], block, ROWS, preferred_element_type=f32)
            outs[j][...] = term.astype(bf16)

    shape = ((left.shape[1], columns), bf16)
    return local_call(kernel, [shape] * GROUP, [owners, left, right])


def scatter_pieces(pieces):
    sent, kept = pieces
    total = kept + exchange(sent, "img", 1).astype(f32)
    result = total[0]
    for digit in range(1, total.shape[0]):
        moved = exchange(total[digit].astype(bf16), "img", 2 * digit)
        result = result + moved.astype(f32)
    return result


def spread_columns(owners, parts, repeats):
    rows, total = parts[0].shape
    size = total // repeats

    def kernel(owner_ref, *refs):
        for j in range(GROUP):
            for r in range(repeats):
                start = pl.multiple_of((r * GROUP + owner_ref[j]) * size, size)
                value = refs[j][:, r * size : (r + 1) * size].astype(f32)
                refs[GROUP][:, pl.ds(start, size)] = value

    return local_call(kernel, [((rows, total * GROUP), f32)], [owners, *parts])[0]


def spread_rows(owners, parts):
    rows, columns = parts[0].shape

    def kernel(owner_ref, *refs):
        for j in range(GROUP):
            start = pl.multiple_of(owner_ref[j] * rows, rows)
            refs[GROUP][pl.ds(start, rows), :] = refs[j][...].astype(f32)

    return local_call(kernel, [((rows * GROUP, columns), f32)], [owners, *parts])[0]


def generic_device(
    tokens,
    classes,
    source_index,
    position_table,
    input_weight,
    query_bias,
    value_bias,
    output_weight,
    output_bias,
    up_weight,
    up_bias,
    down_weight,
    down_bias,
    first_gain,
    first_shift,
    second_gain,
    second_shift,
    cotangent,
):
    shard_rows, width = tokens.shape
    group_slots = shard_rows * GROUP
    size = lax.axis_size("img")
    img, seq = lax.axis_index("img"), lax.axis_index("seq")
    held = width // size
    part = width // GROUP
    heads = HEADS // GROUP
    hidden_units = up_weight.shape[1]
    units = hidden_units // size // GROUP
    scale = HEAD_DIM ** (-0.5)

    input_part = mine_of(input_weight.reshape(held, 3, GROUP, part), seq, 2).reshape(held, 3 * part)
    output_part = mine_of(output_weight.reshape(held, GROUP, part), seq, 1)
    up_part = mine_of(up_weight.reshape(held, size, GROUP, units), seq, 2).reshape(held, size * units)
    down_part = mine_of(down_weight.reshape(GROUP, units, width), seq, 0)
    input_full = place(gather_relative(input_part), img).reshape(width, 3 * part)
    output_cols = place(gather_relative(output_part), img).reshape(GROUP, part, part)
    up_full = place(gather_relative(up_part), img).reshape(width, size * units)
    down_full = place(gather_relative(down_part), img).reshape(size * units, width)
    output_blocks = [mine_of(output_cols, seq, 0)] + [
        exchange(mine_of(output_cols, seq ^ j, 0), "seq", j) for j in range(1, GROUP)
    ]
    output_full = jnp.concatenate(reorder(output_blocks, seq), axis=1)
    query_bias_part = mine_of(query_bias.reshape(GROUP, part), seq, 0)
    value_bias_part = mine_of(value_bias.reshape(GROUP, part), seq, 0)
    up_bias_part = mine_of(up_bias.reshape(size, GROUP, units), seq, 1).reshape(size * units)

    my_slots = seq * shard_rows + jnp.arange(shard_rows, dtype=jnp.int32)
    _, valid, mixing = table_mixing(classes, my_slots, source_index)
    owners = seq ^ jnp.arange(GROUP, dtype=jnp.int32)
    all_slots = (owners[:, None] * shard_rows + jnp.arange(shard_rows, dtype=jnp.int32)[None]).reshape(-1)
    all_segments, _ = slot_segments(classes, all_slots)
    same_image = all_segments[:, None] == all_segments[None, :]

    upstream = jnp.where(valid[:, None], cotangent.astype(f32), 0.0)
    upstream_all = jnp.concatenate(group_gather(upstream.astype(bf16)), axis=0)

    embedded = tokens.astype(f32) + jnp.dot(mixing, position_table, precision=highest)
    first_value, first_pull = jax.vjp(layer_norm, embedded, first_gain, first_shift)
    normed_all = jnp.concatenate(group_gather(first_value.astype(bf16)), axis=0)
    projected = jnp.dot(normed_all, input_full, preferred_element_type=f32)

    def split_heads(value):
        return value.astype(bf16).reshape(group_slots, heads, HEAD_DIM)

    queries = split_heads(projected[:, :part] + query_bias_part)
    keys = split_heads(projected[:, part : 2 * part])
    values = split_heads(projected[:, 2 * part :] + value_bias_part)
    raw_scores = jnp.einsum("qhd,khd->hqk", queries, keys, preferred_element_type=f32)
    logits = jnp.where(same_image[None], raw_scores * scale, masked_value)
    row_max = jnp.max(logits, axis=-1, keepdims=True)
    log_total = row_max + jnp.log(jnp.sum(jnp.exp(logits - row_max), axis=-1, keepdims=True))
    probs = jnp.exp(logits - log_total)
    probs_low = probs.astype(bf16)
    attended = (
        jnp.einsum("hqk,khd->qhd", probs_low, values, preferred_element_type=f32)
        .reshape(group_slots, part)
        .astype(bf16)
    )

    def row_parts(value):
        return [value[j * shard_rows : (j + 1) * shard_rows] for j in range(GROUP)]

    branch_one = group_scatter(row_parts(jnp.dot(attended, output_full, preferred_element_type=f32)))
    hidden = embedded + branch_one + output_bias
    second_value, second_pull = jax.vjp(layer_norm, hidden, second_gain, second_shift)
    second_all = jnp.concatenate(group_gather(second_value.astype(bf16)), axis=0)
    upper = jnp.dot(second_all, up_full, preferred_element_type=f32) + up_bias_part
    active, gelu_pull = jax.vjp(exact_gelu, upper)
    active_low = active.astype(bf16)

    def to_owners(term, rows):
        pieces = term.reshape(size, rows, term.shape[1])
        return scatter_relative([mine_of(pieces, img ^ j, 0) for j in range(size)])

    def columns_of_all(total):
        return reorder(group_gather(total.astype(bf16)), seq)

    down_sum = to_owners(
        jnp.einsum("sf,sd->fd", active_low, upstream_all, preferred_element_type=f32), units
    )
    active_grad = jnp.einsum("sd,fd->sf", upstream_all, down_full, preferred_element_type=f32)
    upper_low = gelu_pull(active_grad)[0].astype(bf16)
    second_grad = group_scatter(
        row_parts(jnp.einsum("sf,df->sd", upper_low, up_full, preferred_element_type=f32))
    )
    up_sum = to_owners(
        jnp.einsum("sd,sf->df", second_all, upper_low, preferred_element_type=f32), held
    )
    branch_two = group_scatter(row_parts(jnp.dot(active_low, down_full, preferred_element_type=f32)))
    block_out = jnp.where(valid[:, None], hidden + branch_two + down_bias, 0.0).astype(bf16)

    hidden_grad, second_gain_grad, second_shift_grad = second_pull(second_grad)
    hidden_grad = hidden_grad + upstream
    branch_low = hidden_grad.astype(bf16)
    branch_all = jnp.concatenate(group_gather(branch_low), axis=0)
    output_term = jnp.einsum("sc,sd->cd", attended, branch_all, preferred_element_type=f32)
    output_term = output_term.astype(bf16).reshape(part, GROUP, part)
    term_blocks = [mine_of(output_term, seq, 1)] + [
        exchange(mine_of(output_term, seq ^ j, 1), "seq", j) for j in range(1, GROUP)
    ]
    output_sum = to_owners(jnp.concatenate(reorder(term_blocks, seq), axis=0).astype(f32), held)

    attended_grad = jnp.einsum(
        "sd,cd->sc", branch_all, output_full, preferred_element_type=f32
    )
    attended_grad = split_heads(attended_grad)
    probs_grad = jnp.einsum("qhd,khd->hqk", attended_grad, values, preferred_element_type=f32)
    inner = jnp.sum(probs * probs_grad, axis=-1, keepdims=True)
    score_low = (scale * (probs * (probs_grad - inner))).astype(bf16)
    query_grad = jnp.einsum("hqk,khd->qhd", score_low, keys, preferred_element_type=f32)
    key_grad = jnp.einsum("hqk,qhd->khd", score_low, queries, preferred_element_type=f32)
    value_grad = jnp.einsum("hqk,qhd->khd", probs_low, attended_grad, preferred_element_type=f32)
    projection_grad = jnp.concatenate(
        [grad.reshape(group_slots, part).astype(bf16) for grad in (query_grad, key_grad, value_grad)],
        axis=1,
    )
    input_sum = to_owners(
        jnp.einsum("sd,se->de", normed_all, projection_grad, preferred_element_type=f32), held
    )
    normed_grad = group_scatter(
        row_parts(jnp.einsum("se,de->sd", projection_grad, input_full, preferred_element_type=f32))
    )
    embedded_grad, first_gain_grad, first_shift_grad = first_pull(normed_grad)
    embedded_grad = embedded_grad + hidden_grad
    table_term = jnp.einsum("st,sd->td", mixing, embedded_grad, precision=highest)

    input_columns = [c.reshape(held, 3, part) for c in columns_of_all(input_sum)]
    input_weight_grad = jnp.stack(input_columns, axis=2).reshape(held, 3 * width).astype(f32)
    output_weight_grad = jnp.concatenate(columns_of_all(output_sum), axis=1).astype(f32)
    up_columns = [c.reshape(held, size, units) for c in columns_of_all(up_sum)]
    up_weight_grad = jnp.stack(up_columns, axis=2).reshape(held, hidden_units).astype(f32)
    down_weight_grad = jnp.concatenate(columns_of_all(down_sum), axis=0).astype(f32)

    def spread(value, shape, axis):
        value = jnp.expand_dims(value.reshape(shape), axis)
        mask = jnp.arange(GROUP, dtype=jnp.int32).reshape([-1 if a == axis else 1 for a in range(value.ndim)])
        return jnp.where(mask == seq, value, 0.0).reshape(-1)

    def columns(value):
        return jnp.sum(value.astype(f32), axis=0)

    projection_sums = columns(projection_grad)
    rows = [
        table_term,
        spread(projection_sums[:part], (part,), 0),
        spread(projection_sums[2 * part :], (part,), 0),
        columns(branch_low),
        columns(upstream),
        first_gain_grad,
        first_shift_grad,
        second_gain_grad,
        second_shift_grad,
        spread(columns(upper_low), (size, units), 1),
    ]
    packed = jnp.concatenate([row.reshape(-1, width) for row in rows])
    used = packed.shape[0]
    packed = jnp.pad(packed, ((0, -used % 32), (0, 0)))
    total = sum_everywhere(packed)
    vectors = total[TABLE:used]
    return (
        block_out,
        embedded_grad.astype(bf16),
        total[:TABLE],
        input_weight_grad,
        vectors[0],
        vectors[1],
        output_weight_grad,
        vectors[2],
        up_weight_grad,
        vectors[8:].reshape(-1),
        down_weight_grad,
        vectors[3],
        vectors[4],
        vectors[5],
        vectors[6],
        vectors[7],
    )


def on_device(
    tokens,
    classes,
    source_index,
    position_table,
    input_weight,
    query_bias,
    value_bias,
    output_weight,
    output_bias,
    up_weight,
    up_bias,
    down_weight,
    down_bias,
    first_gain,
    first_shift,
    second_gain,
    second_shift,
    cotangent,
):
    if up_weight.shape[1] // lax.axis_size("img") // GROUP % 128:
        return generic_device(
            tokens,
            classes,
            source_index,
            position_table,
            input_weight,
            query_bias,
            value_bias,
            output_weight,
            output_bias,
            up_weight,
            up_bias,
            down_weight,
            down_bias,
            first_gain,
            first_shift,
            second_gain,
            second_shift,
            cotangent,
        )
    shard_rows, width = tokens.shape
    size = lax.axis_size("img")
    img, seq = lax.axis_index("img"), lax.axis_index("seq")
    held = width // size
    part = width // GROUP
    hidden_units = up_weight.shape[1]
    units = hidden_units // size // GROUP
    relatives = img ^ jnp.arange(size, dtype=jnp.int32)
    owners = seq ^ jnp.arange(GROUP, dtype=jnp.int32)
    seq_vector = seq[None].astype(jnp.int32)

    blocks = [(0, 1, t * width, 0, t * part, part) for t in range(2)]
    blocks += [(0, 1, 2 * width, 1, 0, part), (1, 1, 0, 1, part, part)]
    first_part, second_part = pick(
        [input_weight, output_weight], blocks, [(held, 2 * part)] * 2, seq_vector
    )
    first_parts = gather_relative(first_part)
    second_parts = gather_relative(second_part)
    blocks = [(0, 1, i * GROUP * units, 0, i * units, units) for i in range(size)]
    up_part, down_part = pick(
        [up_weight, down_weight],
        blocks + [(1, 0, 0, 1, 0, units)],
        [(held, size * units), (units, width)],
        seq_vector,
    )
    up_parts = gather_relative(up_part)
    down_parts = gather_relative(down_part)

    query_bias_part = mine_of(query_bias.reshape(GROUP, part), seq, 0)
    value_bias_part = mine_of(value_bias.reshape(GROUP, part), seq, 0)
    up_bias_part = mine_of(up_bias.reshape(size, GROUP, units), seq, 1).reshape(size * units)

    my_slots = seq * shard_rows + jnp.arange(shard_rows, dtype=jnp.int32)
    _, valid, mixing = table_mixing(classes, my_slots, source_index)
    all_slots = owners[:, None] * shard_rows + jnp.arange(shard_rows, dtype=jnp.int32)[None]
    all_segments, _ = slot_segments(classes, all_slots.reshape(-1))

    embedded = tokens.astype(f32) + jnp.dot(mixing, position_table, precision=highest)
    first_value, first_pull = jax.vjp(layer_norm, embedded, first_gain, first_shift)
    normed_all = jnp.concatenate(group_gather(first_value.astype(bf16)), axis=0)
    upstream = jnp.where(valid[:, None], cotangent.astype(f32), 0.0)
    upstream_all = jnp.concatenate(group_gather(upstream.astype(bf16)), axis=0)

    input_full, output_cols, queries, keys, values, attended, totals = attention_forward(
        relatives, normed_all, first_parts, second_parts, query_bias_part, value_bias_part, all_segments
    )
    attended = attended.reshape(GROUP * shard_rows, part)
    output_cols = output_cols.reshape(GROUP, part, part)
    output_blocks = [mine_of(output_cols, seq, 0)] + [
        exchange(mine_of(output_cols, seq ^ j, 0), "seq", j) for j in range(1, GROUP)
    ]
    output_full = jnp.concatenate(reorder(output_blocks, seq), axis=1)

    def row_parts(value):
        return [value[j * shard_rows : (j + 1) * shard_rows] for j in range(GROUP)]

    branch_one = group_scatter(
        row_parts(jnp.dot(attended, output_full, preferred_element_type=f32))
    )
    hidden = embedded + branch_one + output_bias
    second_value, second_pull = jax.vjp(layer_norm, hidden, second_gain, second_shift)
    second_rows = group_gather(second_value.astype(bf16))
    up_full, second_all, active, slope = feed_forward(relatives, second_rows, up_parts, up_bias_part)
    second_all = second_all.reshape(GROUP * shard_rows, width)
    active = active.reshape(GROUP * shard_rows, size * units)

    down_sum = scatter_pieces(weight_pieces(relatives, active, upstream_all))
    down_full, upper_low, upper_sums, sent, kept = feed_backward(
        relatives, upstream_all.reshape(GROUP, shard_rows, width), down_parts, slope, up_full
    )
    upper_low = upper_low.reshape(GROUP * shard_rows, size * units)
    beside = exchange(sent, "seq", 1)
    far = kept[0] + beside[0].astype(f32)
    second_grad = kept[1] + beside[1].astype(f32)
    second_grad += exchange(far.astype(bf16), "seq", 2).astype(f32)
    up_sum = scatter_pieces(weight_pieces(relatives, second_all, upper_low))
    branch_two = group_scatter(row_parts(jnp.dot(active, down_full, preferred_element_type=f32)))
    block_out = jnp.where(valid[:, None], hidden + branch_two + down_bias, 0.0).astype(bf16)

    hidden_grad, second_gain_grad, second_shift_grad = second_pull(second_grad)
    hidden_grad = hidden_grad + upstream
    branch_low = hidden_grad.astype(bf16)
    branch_all = jnp.concatenate(group_gather(branch_low), axis=0)
    mixed_grad = jnp.einsum("sd,cd->sc", branch_all, output_full, preferred_element_type=f32)
    projection_grad, projection_sums = attention_backward(
        queries, keys, values, mixed_grad.astype(bf16), totals, all_segments
    )
    projection_sums = projection_sums[0]

    term_blocks = group_terms(owners, attended, branch_all)
    term_blocks = [term_blocks[0]] + [exchange(term_blocks[j], "seq", j) for j in range(1, GROUP)]
    per_group = size // GROUP
    stacked = jnp.stack(term_blocks).reshape(size, held, part)
    pieces = [
        mine_of(stacked, ((img ^ j) // per_group ^ seq) * per_group + (img ^ j) % per_group, 0)
        for j in range(size)
    ]
    output_sum = scatter_pieces((jnp.stack(pieces[1::2]), jnp.stack(pieces[0::2]).astype(f32)))

    normed_grad = group_scatter(
        row_parts(jnp.einsum("se,de->sd", projection_grad, input_full, preferred_element_type=f32)),
    )
    input_sum = scatter_pieces(weight_pieces(relatives, normed_all, projection_grad))
    embedded_grad, first_gain_grad, first_shift_grad = first_pull(normed_grad)
    embedded_grad = embedded_grad + hidden_grad
    table_term = jnp.einsum("st,sd->td", mixing, embedded_grad, precision=highest)

    feed_shares = group_gather(jnp.stack([up_sum.astype(bf16), down_sum.astype(bf16)]))
    up_weight_grad = spread_columns(owners, [share[0] for share in feed_shares], size)
    down_weight_grad = spread_rows(owners, [share[1] for share in feed_shares])
    output_weight_grad = spread_columns(owners, group_gather(output_sum.astype(bf16)), 1)
    input_weight_grad = spread_columns(owners, group_gather(input_sum.astype(bf16)), 3)

    def spread(value, shape, axis):
        value = jnp.expand_dims(value.reshape(shape), axis)
        mask = jnp.arange(GROUP, dtype=jnp.int32).reshape([-1 if a == axis else 1 for a in range(value.ndim)])
        return jnp.where(mask == seq, value, 0.0).reshape(-1)

    def columns(value):
        return jnp.sum(value.astype(f32), axis=0)

    rows = [
        table_term,
        spread(projection_sums[:part], (part,), 0),
        spread(projection_sums[2 * part :], (part,), 0),
        columns(branch_low),
        columns(upstream),
        first_gain_grad,
        first_shift_grad,
        second_gain_grad,
        second_shift_grad,
        spread(upper_sums[0], (size, units), 1),
    ]
    packed = jnp.concatenate([row.reshape(-1, width) for row in rows])
    used = packed.shape[0]
    packed = jnp.pad(packed, ((0, -used % 32), (0, 0)))
    total = sum_everywhere(packed)
    vectors = total[TABLE:used]
    return (
        block_out,
        embedded_grad.astype(bf16),
        total[:TABLE],
        input_weight_grad,
        vectors[0],
        vectors[1],
        output_weight_grad,
        vectors[2],
        up_weight_grad,
        vectors[8:].reshape(-1),
        down_weight_grad,
        vectors[3],
        vectors[4],
        vectors[5],
        vectors[6],
        vectors[7],
    )


def solution(mesh):
    placed = (
        P(("img", "seq"), None),
        P("img"),
        P(),
        P(),
        P("img", None),
        P(),
        P(),
        P("img", None),
        P(),
        P("img", None),
        P(),
        P("img", None),
        P(),
        P(),
        P(),
        P(),
        P(),
        P(("img", "seq"), None),
    )
    return jax.shard_map(
        on_device,
        mesh=mesh,
        in_specs=placed,
        out_specs=(
            P(("img", "seq"), None),
            P(("img", "seq"), None),
            P(),
            P("img", None),
            P(),
            P(),
            P("img", None),
            P(),
            P("img", None),
            P(),
            P("img", None),
            P(),
            P(),
            P(),
            P(),
            P(),
        ),
        check_vma=False,
    )
```

profile of v0, /device:TPU:1, one launch (start us, length us, event | category | flops | bytes accessed | tf_op | source)
XLA Modules:
  0.0 391.7 jit_solution(11076196312843329171)
XLA Ops:
  16.4 3.6 collective-permute-start
  30.5 5.3 %collective-permute-done.13.refs_12_ = bf16[128,512]{1,0:T(8,128)(2,1)S(1)} collective-permute-done((bf16[128,512]{1,0:T(8,128)(2,1)S(1)}, bf16[128,512]{1,0:T(8,128)(2,1)S(1)}, u32[]{:S(2)}, u32[]{:S(2)}) %collective-permute-start.13) | collective-permute-done | bytes 131104 | tf_op jit(solution)/shard_map/ppermute | solution.py:80
  51.4 12.6 %shard_map.298 = (bf16[1024,768]{1,0:T(8,128)(2,1)}, bf16[1024,256]{1,0:T(8,128)(2,1)}, bf16[4,152,256]{2,1,0:T(8,128)(2,1)}, bf16[608,256]{1,0:T(8,128)(2,1)}, ...) custom-call(s32[8]{0:T(128)} %iota_xor_fusion.1.index_ref, ...), custom_call_target="tpu_custom_call" | custom-call | tf_op jit(solution)/shard_map/pallas_call | solution.py:200
  65.2 3.4 collective-permute-start.19
  69.1 3.7 collective-permute-done.19
  81.3 2.9 collective-permute-start.38
  89.2 4.7 %collective-permute-done.36.refs_2_ = bf16[128,1024]{1,0:T(8,128)(2,1)S(1)} collective-permute-done((bf16[128,1024]{1,0:T(8,128)(2,1)}, bf16[128,1024]{1,0:T(8,128)(2,1)S(1)}, u32[]{:S(2)}, u32[]{:S(2)}) %collective-permute-start.36) | collective-permute-done | bytes 262176 | tf_op jit(solution)/shard_map/ppermute | solution.py:80
  95.1 6.7 %collective-permute-done.40.refs_6_ = bf16[128,1024]{1,0:T(8,128)(2,1)S(1)} collective-permute-done((bf16[128,1024]{1,0:T(8,128)(2,1)}, bf16[128,1024]{1,0:T(8,128)(2,1)S(1)}, u32[]{:S(2)}, u32[]{:S(2)}) %collective-permute-start.40) | collective-permute-done | bytes 262176 | tf_op jit(solution)/shard_map/ppermute | solution.py:80
  101.8 3.8 collective-permute-start.32
  108.8 15.5 %collective-permute-done.28.refs_8_ = bf16[128,1024]{1,0:T(8,128)(2,1)S(1)} collective-permute-done((bf16[128,1024]{1,0:T(8,128)(2,1)S(1)}, bf16[128,1024]{1,0:T(8,128)(2,1)S(1)}, u32[]{:S(2)}, u32[]{:S(2)}) %collective-permute-start.28) | collective-permute-done | bytes 262176 | tf_op jit(solution)/shard_map/ppermute | solution.py:80
  131.1 3.0 collective-permute-start.24
  135.8 5.5 %collective-permute-done.31.refs_11_ = bf16[128,1024]{1,0:T(8,128)(2,1)} collective-permute-done((bf16[128,1024]{1,0:T(8,128)(2,1)S(1)}, bf16[128,1024]{1,0:T(8,128)(2,1)}, u32[]{:S(2)}, u32[]{:S(2)}) %collective-permute-start.31) | collective-permute-done | bytes 262176 | tf_op jit(solution)/shard_map/ppermute | solution.py:80
  146.3 8.8 %shard_map.300 = (bf16[1024,1024]{1,0:T(8,128)(2,1)}, bf16[4,152,1024]{2,1,0:T(8,128)(2,1)}, bf16[4,152,1024]{2,1,0:T(8,128)(2,1)}, f32[4,152,1024]{2,1,0:T(8,128)}) custom-call(s32[8]{0:T(128)} %iota_xor_fusion.1.index_ref, bf16[152,1024]{1,0:T(8,128)(2,1)} %copy-done.13, bf16[152,1024]{1,0:T(8,128)(2,1)} %copy-done.29, bf16[152,1024]{1,0:T(8,128)(2,1)} %copy-done.28, ...), custom_call_target="tpu_custom_call" | custom-call | tf_op jit(solution)/shard_map/pallas_call | solution.py:200
  158.1 5.6 %collective-permute-done.41.refs_7_ = bf16[128,1024]{1,0:T(8,128)(2,1)S(1)} collective-permute-done((bf16[128,1024]{1,0:T(8,128)(2,1)S(1)}, bf16[128,1024]{1,0:T(8,128)(2,1)S(1)}, u32[]{:S(2)}, u32[]{:S(2)}) %collective-permute-start.41) | collective-permute-done | bytes 262176 | tf_op jit(solution)/shard_map/ppermute | solution.py:80
  164.4 10.3 %shard_map.301 = (bf16[1024,1024]{1,0:T(8,128)(2,1)}, bf16[4,152,1024]{2,1,0:T(8,128)(2,1)}, f32[1,1024]{1,0:T(1,128)}, bf16[2,152,1024]{2,1,0:T(8,128)(2,1)}, f32[2,152,1024]{2,1,0:T(8,128)}) custom-call(s32[8]{0:T(128)} %iota_xor_fusion.1.index_ref, bf16[4,152,1024]{2,1,0:T(8,128)(2,1)} %bitcast.212, bf16[128,1024]{1,0:T(8,128)(2,1)} %get-tuple-element.54.refs_0_, ...), custom_call_target="tpu_custom_call" | custom-call | tf_op jit(solution)/shard_map/pallas_call | solution.py:200
  176.0 4.5 %fusion.75 = (bf16[608,1024]{1,0:T(8,128)(2,1)S(1)}, f32[608,1024]{1,0:T(8,128)}) fusion(bf16[608,1024]{1,0:T(8,128)(2,1)S(1)} %bitcast.220, bf16[1024,1024]{1,0:T(8,128)(2,1)} %get-tuple-element.57), kind=kOutput, calls=%fused_computation.211 | convolution fusion | flops 1275691008 | bytes 7077888 | tf_op jit(solution)/shard_map/dot_general | solution.py:800
  183.9 4.9 %shard_map.308 = (bf16[4,128,1024]{2,1,0:T(8,128)(2,1)}, f32[4,128,1024]{2,1,0:T(8,128)}) custom-call(s32[8]{0:T(128)} %iota_xor_fusion.1.index_ref, bf16[608,1024]{1,0:T(8,128)(2,1)} %bitcast.219, bf16[608,1024]{1,0:T(8,128)(2,1)} %pad_maximum_fusion.1.right_ref), custom_call_target="tpu_custom_call" | custom-call | tf_op jit(solution)/shard_map/pallas_call | solution.py:200
  188.8 5.1 %shard_map.307 = (bf16[4,128,1024]{2,1,0:T(8,128)(2,1)}, f32[4,128,1024]{2,1,0:T(8,128)}) custom-call(s32[8]{0:T(128)} %iota_xor_fusion.1.index_ref, bf16[608,1024]{1,0:T(8,128)(2,1)} %bitcast.218, bf16[608,1024]{1,0:T(8,128)(2,1)} %bitcast.221), custom_call_target="tpu_custom_call" | custom-call | tf_op jit(solution)/shard_map/pallas_call | solution.py:200
  199.3 4.8 %collective-permute-done.43 = bf16[152,1024]{1,0:T(8,128)(2,1)S(1)} collective-permute-done((bf16[152,1024]{1,0:T(8,128)(2,1)S(1)}, bf16[152,1024]{1,0:T(8,128)(2,1)S(1)}, u32[]{:S(2)}, u32[]{:S(2)}) %collective-permute-start.43) | collective-permute-done | bytes 311328 | tf_op jit(solution)/shard_map/ppermute | solution.py:80
  210.4 7.7 %collective-permute-done.76 = bf16[4,128,1024]{2,1,0:T(8,128)(2,1)S(1)} collective-permute-done((bf16[4,128,1024]{2,1,0:T(8,128)(2,1)}, bf16[4,128,1024]{2,1,0:T(8,128)(2,1)S(1)}, u32[]{:S(2)}, u32[]{:S(2)}) %collective-permute-start.76) | collective-permute-done | bytes 1048608 | tf_op jit(solution)/shard_map/ppermute | solution.py:80
  221.3 3.0 collective-permute-start.78
  224.4 16.2 %collective-permute-done.80 = bf16[4,128,1024]{2,1,0:T(8,128)(2,1)S(1)} collective-permute-done((bf16[4,128,1024]{2,1,0:T(8,128)(2,1)}, bf16[4,128,1024]{2,1,0:T(8,128)(2,1)S(1)}, u32[]{:S(2)}, u32[]{:S(2)}) %collective-permute-start.80) | collective-permute-done | bytes 1048608 | tf_op jit(solution)/shard_map/ppermute | solution.py:80
  240.6 4.4 %collective-permute-start.77 = (bf16[128,1024]{1,0:T(8,128)(2,1)S(1)}, bf16[128,1024]{1,0:T(8,128)(2,1)S(1)}, u32[]{:S(2)}, u32[]{:S(2)}) collective-permute-start(bf16[128,1024]{1,0:T(8,128)(2,1)S(1)} %get-tuple-element.120), channel_id=1, source_target_pairs={{0,8},{4,12},{8,0},{12,4},{16,24},{20,28},{24,16},{28,20},{1,9},{5... | collective-permute-start | bytes 786440 | tf_op jit(solution)/shard_map/ppermute | solution.py:80
  250.0 8.3 %collective-permute-start.48 = (bf16[152,1024]{1,0:T(8,128)(2,1)S(1)}, bf16[152,1024]{1,0:T(8,128)(2,1)S(1)}, u32[]{:S(2)}, u32[]{:S(2)}) collective-permute-start(bf16[152,1024]{1,0:T(8,128)(2,1)S(1)} %collective-permute-done.47), channel_id=1, source_target_pairs={{0,1},{1,0},{2,3},{3,2},{4,5},{5,4},{6,7},{7,6},{8,9},{9,8},{10,11... | collective-permute-start | bytes 933896 | tf_op jit(solution)/shard_map/ppermute | solution.py:80
  258.6 9.8 %collective-permute-done.82 = bf16[128,1024]{1,0:T(8,128)(2,1)S(1)} collective-permute-done((bf16[128,1024]{1,0:T(8,128)(2,1)S(1)}, bf16[128,1024]{1,0:T(8,128)(2,1)S(1)}, u32[]{:S(2)}, u32[]{:S(2)}) %collective-permute-start.82) | collective-permute-done | bytes 262176 | tf_op jit(solution)/shard_map/ppermute | solution.py:80
  272.0 13.4 %shard_map.302 = (bf16[608,768]{1,0:T(8,128)(2,1)}, f32[1,768]{1,0:T(1,128)}) custom-call(s32[1]{0:T(128)} %constant.234.clone.1.zero_ref, bf16[4,152,256]{2,1,0:T(8,128)(2,1)} %get-tuple-element.58.q_ref, bf16[608,256]{1,0:T(8,128)(2,1)} %get-tuple-element.59.k_ref, bf16[608,256]{1,0:T(8,128)(2,1)} %get-tuple-element.60.v_ref, ...), custom_call_target="tpu_custom_call" | custom-call | tf_op jit(solution)/shard_map/pallas_call | solution.py:200
  297.1 4.2 %shard_map.303 = (bf16[4,128,768]{2,1,0:T(8,128)(2,1)}, f32[4,128,768]{2,1,0:T(8,128)}) custom-call(s32[8]{0:T(128)} %iota_xor_fusion.1.index_ref, bf16[608,1024]{1,0:T(8,128)(2,1)} %pad_maximum_fusion.x_ref.left_ref, bf16[608,768]{1,0:T(8,128)(2,1)} %get-tuple-element.64.right_ref), custom_call_target="tpu_custom_call" | custom-call | tf_op jit(solution)/shard_map/pallas_call | solution.py:200
  307.4 21.0 %collective-permute-done.69 = bf16[4,128,256]{2,1,0:T(8,128)(2,1)S(1)} collective-permute-done((bf16[4,128,256]{2,1,0:T(8,128)(2,1)S(1)}, bf16[4,128,256]{2,1,0:T(8,128)(2,1)S(1)}, u32[]{:S(2)}, u32[]{:S(2)}) %collective-permute-start.69) | collective-permute-done | bytes 262176 | tf_op jit(solution)/shard_map/ppermute | solution.py:80
  350.2 6.2 %collective-permute-start.55 = (f32[16,1024]{1,0:T(8,128)S(1)}, f32[16,1024]{1,0:T(8,128)S(1)}, u32[]{:S(2)}, u32[]{:S(2)}) collective-permute-start(f32[16,1024]{1,0:T(8,128)S(1)} %add.501), channel_id=1, source_target_pairs={{0,16},{4,20},{8,24},{12,28},{16,0},{20,4},{24,8},{28,12},{1,17},{... | collective-permute-start | bytes 196616 | tf_op jit(solution)/shard_map/ppermute | solution.py:80
  356.4 4.6 %collective-permute-done.61 = bf16[128,768]{1,0:T(8,128)(2,1)S(1)} collective-permute-done((bf16[128,768]{1,0:T(8,128)(2,1)S(1)}, bf16[128,768]{1,0:T(8,128)(2,1)S(1)}, u32[]{:S(2)}, u32[]{:S(2)}) %collective-permute-start.61) | collective-permute-done | bytes 196640 | tf_op jit(solution)/shard_map/ppermute | solution.py:80
  363.3 4.1 %collective-permute-start.86 = (bf16[2,128,1024]{2,1,0:T(8,128)(2,1)S(1)}, bf16[2,128,1024]{2,1,0:T(8,128)(2,1)S(1)}, u32[]{:S(2)}, u32[]{:S(2)}) collective-permute-start(bf16[2,128,1024]{2,1,0:T(8,128)(2,1)S(1)} %copy-done.17), channel_id=1, source_target_pairs={{0,1},{1,0},{2,3},{3,2},{4,5},{5,4},{6,7},{7,6},{8,9},{9,8},{10,11... | collective-permute-start | bytes 1572872 | tf_op jit(solution)/shard_map/ppermute | solution.py:80
  367.5 3.2 collective-permute-start.75
  (424 shorter events, 168.7 us)
Async XLA Ops:
  16.4 21.2 %collective-permute-start = (bf16[152,1024]{1,0:T(8,128)(2,1)S(1)}, bf16[152,1024]{1,0:T(8,128)(2,1)S(1)}, u32[]{:S(2)}, u32[]{:S(2)}) collective-permute-start(bf16[152,1024]{1,0:T(8,128)(2,1)S(1)} %add_convert_fusion.2), channel_id=1, source_target_pairs={{0,1},{1,0},{2,3},{3,2},{4,5},{5,4},{6,7},{7,6},{8,9},{9,8},{10,11... | collective-permute-start | bytes 933896 | tf_op jit(solution)/shard_map/ppermute | solution.py:80
  21.5 17.3 %collective-permute-start.2 = (bf16[152,1024]{1,0:T(8,128)(2,1)S(1)}, bf16[152,1024]{1,0:T(8,128)(2,1)S(1)}, u32[]{:S(2)}, u32[]{:S(2)}) collective-permute-start(bf16[152,1024]{1,0:T(8,128)(2,1)S(1)} %collective-permute-done.1), channel_id=1, source_target_pairs={{0,1},{1,0},{2,3},{3,2},{4,5},{5,4},{6,7},{7,6},{8,9},{9,8},{10,11... | collective-permute-start | bytes 933896 | tf_op jit(solution)/shard_map/ppermute | solution.py:80
  84.2 17.6 %collective-permute-start.40 = (bf16[128,1024]{1,0:T(8,128)(2,1)}, bf16[128,1024]{1,0:T(8,128)(2,1)S(1)}, u32[]{:S(2)}, u32[]{:S(2)}) collective-permute-start(bf16[128,1024]{1,0:T(8,128)(2,1)} %get-tuple-element.54.refs_0_), channel_id=1, source_target_pairs={{0,24},{4,28},{8,16},{12,20},{16,8},{20,12},{24,0},{28,4},{1,25},{... | collective-permute-start | bytes 786440 | tf_op jit(solution)/shard_map/ppermute | solution.py:80
  84.6 21.1 %collective-permute-start.25 = (bf16[128,1024]{1,0:T(8,128)(2,1)}, bf16[128,1024]{1,0:T(8,128)(2,1)S(1)}, u32[]{:S(2)}, u32[]{:S(2)}) collective-permute-start(bf16[128,1024]{1,0:T(8,128)(2,1)} %get-tuple-element.52.refs_4_), channel_id=1, source_target_pairs={{0,4},{4,0},{8,12},{12,8},{16,20},{20,16},{24,28},{28,24},{1,5},{5... | collective-permute-start | bytes 786440 | tf_op jit(solution)/shard_map/ppermute | solution.py:80
  87.4 20.9 %collective-permute-start.26 = (bf16[128,1024]{1,0:T(8,128)(2,1)}, bf16[128,1024]{1,0:T(8,128)(2,1)S(1)}, u32[]{:S(2)}, u32[]{:S(2)}) collective-permute-start(bf16[128,1024]{1,0:T(8,128)(2,1)} %get-tuple-element.52.refs_4_), channel_id=1, source_target_pairs={{0,8},{4,12},{8,0},{12,4},{16,24},{20,28},{24,16},{28,20},{1,9},{5... | collective-permute-start | bytes 786440 | tf_op jit(solution)/shard_map/ppermute | solution.py:80
  93.9 30.3 %collective-permute-start.28 = (bf16[128,1024]{1,0:T(8,128)(2,1)S(1)}, bf16[128,1024]{1,0:T(8,128)(2,1)S(1)}, u32[]{:S(2)}, u32[]{:S(2)}) collective-permute-start(bf16[128,1024]{1,0:T(8,128)(2,1)S(1)} %copy-done.40), channel_id=1, source_target_pairs={{0,16},{4,20},{8,24},{12,28},{16,0},{20,4},{24,8},{28,12},{1,17},{... | collective-permute-start | bytes 786440 | tf_op jit(solution)/shard_map/ppermute | solution.py:80
  94.0 31.3 %collective-permute-start.33 = (bf16[152,1024]{1,0:T(8,128)(2,1)S(1)}, bf16[152,1024]{1,0:T(8,128)(2,1)S(1)}, u32[]{:S(2)}, u32[]{:S(2)}) collective-permute-start(bf16[152,1024]{1,0:T(8,128)(2,1)S(1)} %fusion.13), channel_id=1, source_target_pairs={{0,2},{1,3},{2,0},{3,1},{4,6},{5,7},{6,4},{7,5},{8,10},{9,11},{10,... | collective-permute-start | bytes 933896 | tf_op jit(solution)/shard_map/ppermute | solution.py:80
  101.8 26.4 %collective-permute-start.32 = (bf16[152,1024]{1,0:T(8,128)(2,1)S(1)}, bf16[152,1024]{1,0:T(8,128)(2,1)S(1)}, u32[]{:S(2)}, u32[]{:S(2)}) collective-permute-start(bf16[152,1024]{1,0:T(8,128)(2,1)S(1)} %fusion.13), channel_id=1, source_target_pairs={{0,1},{1,0},{2,3},{3,2},{4,5},{5,4},{6,7},{7,6},{8,9},{9,8},{10,11... | collective-permute-start | bytes 933896 | tf_op jit(solution)/shard_map/ppermute | solution.py:80
  105.7 22.4 %collective-permute-start.30 = (bf16[128,1024]{1,0:T(8,128)(2,1)S(1)}, bf16[128,1024]{1,0:T(8,128)(2,1)S(1)}, u32[]{:S(2)}, u32[]{:S(2)}) collective-permute-start(bf16[128,1024]{1,0:T(8,128)(2,1)S(1)} %copy-done.40), channel_id=1, source_target_pairs={{0,24},{4,28},{8,16},{12,20},{16,8},{20,12},{24,0},{28,4},{1,25},{... | collective-permute-start | bytes 786440 | tf_op jit(solution)/shard_map/ppermute | solution.py:80
  108.3 20.1 %collective-permute-start.27 = (bf16[128,1024]{1,0:T(8,128)(2,1)S(1)}, bf16[128,1024]{1,0:T(8,128)(2,1)S(1)}, u32[]{:S(2)}, u32[]{:S(2)}) collective-permute-start(bf16[128,1024]{1,0:T(8,128)(2,1)S(1)} %collective-permute-done.26.refs_6_), channel_id=1, source_target_pairs={{0,4},{4,0},{8,12},{12,8},{16,20},{20,16},{24,28},{28,24},{1,5},{5... | collective-permute-start | bytes 786440 | tf_op jit(solution)/shard_map/ppermute | solution.py:80
  125.3 16.3 %collective-permute-start.34 = (bf16[152,1024]{1,0:T(8,128)(2,1)S(1)}, bf16[152,1024]{1,0:T(8,128)(2,1)S(1)}, u32[]{:S(2)}, u32[]{:S(2)}) collective-permute-start(bf16[152,1024]{1,0:T(8,128)(2,1)S(1)} %collective-permute-done.33), channel_id=1, source_target_pairs={{0,1},{1,0},{2,3},{3,2},{4,5},{5,4},{6,7},{7,6},{8,9},{9,8},{10,11... | collective-permute-start | bytes 933896 | tf_op jit(solution)/shard_map/ppermute | solution.py:80
  135.6 19.5 %collective-permute-start.35 = (bf16[128,1024]{1,0:T(8,128)(2,1)S(1)}, bf16[128,1024]{1,0:T(8,128)(2,1)S(1)}, u32[]{:S(2)}, u32[]{:S(2)}) collective-permute-start(bf16[128,1024]{1,0:T(8,128)(2,1)S(1)} %copy-done.31), channel_id=1, source_target_pairs={{0,4},{4,0},{8,12},{12,8},{16,20},{20,16},{24,28},{28,24},{1,5},{5... | collective-permute-start | bytes 786440 | tf_op jit(solution)/shard_map/ppermute | solution.py:80
  141.6 16.5 %collective-permute-start.39 = (bf16[128,1024]{1,0:T(8,128)(2,1)S(1)}, bf16[128,1024]{1,0:T(8,128)(2,1)S(1)}, u32[]{:S(2)}, u32[]{:S(2)}) collective-permute-start(bf16[128,1024]{1,0:T(8,128)(2,1)S(1)} %collective-permute-done.38.refs_4_), channel_id=1, source_target_pairs={{0,4},{4,0},{8,12},{12,8},{16,20},{20,16},{24,28},{28,24},{1,5},{5... | collective-permute-start | bytes 786440 | tf_op jit(solution)/shard_map/ppermute | solution.py:80
  142.8 20.9 %collective-permute-start.41 = (bf16[128,1024]{1,0:T(8,128)(2,1)S(1)}, bf16[128,1024]{1,0:T(8,128)(2,1)S(1)}, u32[]{:S(2)}, u32[]{:S(2)}) collective-permute-start(bf16[128,1024]{1,0:T(8,128)(2,1)S(1)} %collective-permute-done.40.refs_6_), channel_id=1, source_target_pairs={{0,4},{4,0},{8,12},{12,8},{16,20},{20,16},{24,28},{28,24},{1,5},{5... | collective-permute-start | bytes 786440 | tf_op jit(solution)/shard_map/ppermute | solution.py:80
  193.9 24.2 %collective-permute-start.76 = (bf16[4,128,1024]{2,1,0:T(8,128)(2,1)}, bf16[4,128,1024]{2,1,0:T(8,128)(2,1)S(1)}, u32[]{:S(2)}, u32[]{:S(2)}) collective-permute-start(bf16[4,128,1024]{2,1,0:T(8,128)(2,1)} %get-tuple-element.77), channel_id=1, source_target_pairs={{0,4},{4,0},{8,12},{12,8},{16,20},{20,16},{24,28},{28,24},{1,5},{5... | collective-permute-start | bytes 3145736 | tf_op jit(solution)/shard_map/ppermute | solution.py:80
  194.2 46.4 %collective-permute-start.80 = (bf16[4,128,1024]{2,1,0:T(8,128)(2,1)}, bf16[4,128,1024]{2,1,0:T(8,128)(2,1)S(1)}, u32[]{:S(2)}, u32[]{:S(2)}) collective-permute-start(bf16[4,128,1024]{2,1,0:T(8,128)(2,1)} %get-tuple-element.79), channel_id=1, source_target_pairs={{0,4},{4,0},{8,12},{12,8},{16,20},{20,16},{24,28},{28,24},{1,5},{5... | collective-permute-start | bytes 3145736 | tf_op jit(solution)/shard_map/ppermute | solution.py:80
  206.5 39.0 %collective-permute-start.47 = (bf16[152,1024]{1,0:T(8,128)(2,1)S(1)}, bf16[152,1024]{1,0:T(8,128)(2,1)S(1)}, u32[]{:S(2)}, u32[]{:S(2)}) collective-permute-start(bf16[152,1024]{1,0:T(8,128)(2,1)S(1)} %get-tuple-element.95), channel_id=1, source_target_pairs={{0,2},{1,3},{2,0},{3,1},{4,6},{5,7},{6,4},{7,5},{8,10},{9,11},{10,... | collective-permute-start | bytes 933896 | tf_op jit(solution)/shard_map/ppermute | solution.py:80
  207.9 61.8 %collective-permute-start.46 = (bf16[152,1024]{1,0:T(8,128)(2,1)S(1)}, bf16[152,1024]{1,0:T(8,128)(2,1)S(1)}, u32[]{:S(2)}, u32[]{:S(2)}) collective-permute-start(bf16[152,1024]{1,0:T(8,128)(2,1)S(1)} %get-tuple-element.95), channel_id=1, source_target_pairs={{0,1},{1,0},{2,3},{3,2},{4,5},{5,4},{6,7},{7,6},{8,9},{9,8},{10,11... | collective-permute-start | bytes 933896 | tf_op jit(solution)/shard_map/ppermute | solution.py:80
  218.7 29.1 %collective-permute-start.79 = (bf16[128,1024]{1,0:T(8,128)(2,1)S(1)}, bf16[128,1024]{1,0:T(8,128)(2,1)S(1)}, u32[]{:S(2)}, u32[]{:S(2)}) collective-permute-start(bf16[128,1024]{1,0:T(8,128)(2,1)S(1)} %get-tuple-element.121), channel_id=1, source_target_pairs={{0,24},{4,28},{8,16},{12,20},{16,8},{20,12},{24,0},{28,4},{1,25},{... | collective-permute-start | bytes 786440 | tf_op jit(solution)/shard_map/ppermute | solution.py:80
  221.3 26.5 %collective-permute-start.78 = (bf16[128,1024]{1,0:T(8,128)(2,1)S(1)}, bf16[128,1024]{1,0:T(8,128)(2,1)S(1)}, u32[]{:S(2)}, u32[]{:S(2)}) collective-permute-start(bf16[128,1024]{1,0:T(8,128)(2,1)S(1)} %get-tuple-element.122), channel_id=1, source_target_pairs={{0,16},{4,20},{8,24},{12,28},{16,0},{20,4},{24,8},{28,12},{1,17},{... | collective-permute-start | bytes 786440 | tf_op jit(solution)/shard_map/ppermute | solution.py:80
  247.9 20.6 %collective-permute-start.82 = (bf16[128,1024]{1,0:T(8,128)(2,1)S(1)}, bf16[128,1024]{1,0:T(8,128)(2,1)S(1)}, u32[]{:S(2)}, u32[]{:S(2)}) collective-permute-start(bf16[128,1024]{1,0:T(8,128)(2,1)S(1)} %get-tuple-element.119), channel_id=1, source_target_pairs={{0,16},{4,20},{8,24},{12,28},{16,0},{20,4},{24,8},{28,12},{1,17},{... | collective-permute-start | bytes 786440 | tf_op jit(solution)/shard_map/ppermute | solution.py:80
  247.9 20.6 %collective-permute-start.81 = (bf16[128,1024]{1,0:T(8,128)(2,1)S(1)}, bf16[128,1024]{1,0:T(8,128)(2,1)S(1)}, u32[]{:S(2)}, u32[]{:S(2)}) collective-permute-start(bf16[128,1024]{1,0:T(8,128)(2,1)S(1)} %get-tuple-element.117), channel_id=1, source_target_pairs={{0,8},{4,12},{8,0},{12,4},{16,24},{20,28},{24,16},{28,20},{1,9},{5... | collective-permute-start | bytes 786440 | tf_op jit(solution)/shard_map/ppermute | solution.py:80
  250.0 19.7 %collective-permute-start.48 = (bf16[152,1024]{1,0:T(8,128)(2,1)S(1)}, bf16[152,1024]{1,0:T(8,128)(2,1)S(1)}, u32[]{:S(2)}, u32[]{:S(2)}) collective-permute-start(bf16[152,1024]{1,0:T(8,128)(2,1)S(1)} %collective-permute-done.47), channel_id=1, source_target_pairs={{0,1},{1,0},{2,3},{3,2},{4,5},{5,4},{6,7},{7,6},{8,9},{9,8},{10,11... | collective-permute-start | bytes 933896 | tf_op jit(solution)/shard_map/ppermute | solution.py:80
  269.4 36.2 %collective-permute-start.85 = (bf16[2,128,1024]{2,1,0:T(8,128)(2,1)}, bf16[2,128,1024]{2,1,0:T(8,128)(2,1)S(1)}, u32[]{:S(2)}, u32[]{:S(2)}) collective-permute-start(bf16[2,128,1024]{2,1,0:T(8,128)(2,1)} %pad_maximum_fusion.9), channel_id=1, source_target_pairs={{0,2},{1,3},{2,0},{3,1},{4,6},{5,7},{6,4},{7,5},{8,10},{9,11},{10,... | collective-permute-start | bytes 1572872 | tf_op jit(solution)/shard_map/ppermute | solution.py:80
  287.9 18.6 %collective-permute-start.49 = (bf16[2,152,1024]{2,1,0:T(8,128)(2,1)S(1)}, bf16[2,152,1024]{2,1,0:T(8,128)(2,1)S(1)}, u32[]{:S(2)}, u32[]{:S(2)}) collective-permute-start(bf16[2,152,1024]{2,1,0:T(8,128)(2,1)S(1)} %pad_maximum_fusion.5), channel_id=1, source_target_pairs={{0,1},{1,0},{2,3},{3,2},{4,5},{5,4},{6,7},{7,6},{8,9},{9,8},{10,11... | collective-permute-start | bytes 1867784 | tf_op jit(solution)/shard_map/ppermute | solution.py:80
  301.4 70.1 %collective-permute-start.84 = (bf16[2,128,1024]{2,1,0:T(8,128)(2,1)}, bf16[2,128,1024]{2,1,0:T(8,128)(2,1)}, u32[]{:S(2)}, u32[]{:S(2)}) collective-permute-start(bf16[2,128,1024]{2,1,0:T(8,128)(2,1)} %pad_maximum_fusion.9), channel_id=1, source_target_pairs={{0,1},{1,0},{2,3},{3,2},{4,5},{5,4},{6,7},{7,6},{8,9},{9,8},{10,11... | collective-permute-start | bytes 1572872 | tf_op jit(solution)/shard_map/ppermute | solution.py:80
  303.9 31.2 %collective-permute-start.59 = (bf16[4,128,768]{2,1,0:T(8,128)(2,1)}, bf16[4,128,768]{2,1,0:T(8,128)(2,1)}, u32[]{:S(2)}, u32[]{:S(2)}) collective-permute-start(bf16[4,128,768]{2,1,0:T(8,128)(2,1)} %get-tuple-element.69), channel_id=1, source_target_pairs={{0,4},{4,0},{8,12},{12,8},{16,20},{20,16},{24,28},{28,24},{1,5},{5... | collective-permute-start | bytes 2359304 | tf_op jit(solution)/shard_map/ppermute | solution.py:80
  304.4 24.1 %collective-permute-start.69 = (bf16[4,128,256]{2,1,0:T(8,128)(2,1)S(1)}, bf16[4,128,256]{2,1,0:T(8,128)(2,1)S(1)}, u32[]{:S(2)}, u32[]{:S(2)}) collective-permute-start(bf16[4,128,256]{2,1,0:T(8,128)(2,1)S(1)} %pad_maximum_fusion.10), channel_id=1, source_target_pairs={{0,4},{4,0},{8,12},{12,8},{16,20},{20,16},{24,28},{28,24},{1,5},{5... | collective-permute-start | bytes 786440 | tf_op jit(solution)/shard_map/ppermute | solution.py:80
  306.6 24.9 %collective-permute-start.50 = (bf16[152,1024]{1,0:T(8,128)(2,1)S(1)}, bf16[152,1024]{1,0:T(8,128)(2,1)S(1)}, u32[]{:S(2)}, u32[]{:S(2)}) collective-permute-start(bf16[152,1024]{1,0:T(8,128)(2,1)S(1)} %fusion), channel_id=1, source_target_pairs={{0,2},{1,3},{2,0},{3,1},{4,6},{5,7},{6,4},{7,5},{8,10},{9,11},{10,... | collective-permute-start | bytes 933896 | tf_op jit(solution)/shard_map/ppermute | solution.py:80
  344.8 16.3 %collective-permute-start.61 = (bf16[128,768]{1,0:T(8,128)(2,1)S(1)}, bf16[128,768]{1,0:T(8,128)(2,1)S(1)}, u32[]{:S(2)}, u32[]{:S(2)}) collective-permute-start(bf16[128,768]{1,0:T(8,128)(2,1)S(1)} %get-tuple-element.125), channel_id=1, source_target_pairs={{0,16},{4,20},{8,24},{12,28},{16,0},{20,4},{24,8},{28,12},{1,17},{... | collective-permute-start | bytes 589832 | tf_op jit(solution)/shard_map/ppermute | solution.py:80
  344.9 18.3 %collective-permute-start.60 = (bf16[128,768]{1,0:T(8,128)(2,1)S(1)}, bf16[128,768]{1,0:T(8,128)(2,1)S(1)}, u32[]{:S(2)}, u32[]{:S(2)}) collective-permute-start(bf16[128,768]{1,0:T(8,128)(2,1)S(1)} %get-tuple-element.123), channel_id=1, source_target_pairs={{0,8},{4,12},{8,0},{12,4},{16,24},{20,28},{24,16},{28,20},{1,9},{5... | collective-permute-start | bytes 589832 | tf_op jit(solution)/shard_map/ppermute | solution.py:80
  350.2 17.2 %collective-permute-start.55 = (f32[16,1024]{1,0:T(8,128)S(1)}, f32[16,1024]{1,0:T(8,128)S(1)}, u32[]{:S(2)}, u32[]{:S(2)}) collective-permute-start(f32[16,1024]{1,0:T(8,128)S(1)} %add.501), channel_id=1, source_target_pairs={{0,16},{4,20},{8,24},{12,28},{16,0},{20,4},{24,8},{28,12},{1,17},{... | collective-permute-start | bytes 196616 | tf_op jit(solution)/shard_map/ppermute | solution.py:80
  (134 other events, 1737.9 us)
where the time goes:
time: 393 us; the launch traced here: 392 us
  waiting for transfers between devices  144 us (37%)
  starting transfers between devices  117 us (30%)
  Pallas kernels  75.5 us (19%)
  other arithmetic  24.1 us (6%)
  local copies, waits for them, and re-layouts  18 us (5%)
  matrix products  11.1 us (3%)
    ppermute x87, waiting for transfers between devices, exchange(): return lax.ppermute(value, axis, [(i, i ^ distance) for i in range(size)])  144 us
    ppermute x87, starting transfers between devices, exchange(): return lax.ppermute(value, axis, [(i, i ^ distance) for i in range(size)])  117 us
    pallas_call x12, Pallas kernels, local_call(): pl.pallas_call(kernel, out_shape=[jax.ShapeDtypeStruct(shape, kind) for s...  71.7 us
  transfers between devices with their start and end apart: 87, of which 28 were waited for; matrix products, arithmetic and copies ran while one was open for 11% of the time, Pallas kernels for 13%

commit v1 on v0

--- a/solution.py
+++ b/solution.py
@@ -70,6 +70,7 @@
     return (segment, valid, mixing)
 
 
+IMG, SEQ = "img", "seq"
 GROUP = 4
 f32 = jnp.float32
 bf16 = jnp.bfloat16
@@ -91,17 +92,17 @@
 
 def gather_relative(shard):
     parts = {0: shard}
-    for stride, radix in phases(lax.axis_size("img")):
+    for stride, radix in phases(lax.axis_size(IMG)):
         held = dict(parts)
         if len(held) <= 4:
             for j, part in held.items():
                 for digit in range(1, radix):
-                    parts[j ^ (digit * stride)] = exchange(part, "img", digit * stride)
+                    parts[j ^ (digit * stride)] = exchange(part, IMG, digit * stride)
         else:
             order = sorted(held)
             stacked = jnp.stack([held[j] for j in order])
             for digit in range(1, radix):
-                received = exchange(stacked, "img", digit * stride)
+                received = exchange(stacked, IMG, digit * stride)
                 for position, j in enumerate(order):
                     parts[j ^ (digit * stride)] = received[position]
     return [parts[j] for j in range(len(parts))]
@@ -109,7 +110,7 @@
 
 def scatter_relative(pieces):
     held = {j: piece for j, piece in enumerate(pieces)}
-    for stride, radix in reversed(phases(lax.axis_size("img"))):
+    for stride, radix in reversed(phases(lax.axis_size(IMG))):
         keep = sorted(j for j in held if (j // stride) % radix == 0)
         total = {j: held[j] for j in keep}
         order = [j for j in keep if j != 0] + [0]
@@ -117,11 +118,11 @@
             for j in order:
                 for digit in range(1, radix):
                     sent = held[j + digit * stride].astype(bf16)
-                    total[j] = total[j] + exchange(sent, "img", digit * stride).astype(f32)
+                    total[j] = total[j] + exchange(sent, IMG, digit * stride).astype(f32)
         else:
             for digit in range(1, radix):
                 sent = jnp.stack([held[j + digit * stride].astype(bf16) for j in keep])
-                received = exchange(sent, "img", digit * stride)
+                received = exchange(sent, IMG, digit * stride)
                 for position, j in enumerate(keep):
                     total[j] = total[j] + received[position].astype(f32)
         held = total
@@ -129,16 +130,21 @@
 
 
 def group_gather(value):
-    across = exchange(value, "seq", 2)
-    beside = exchange(value, "seq", 1)
-    return [value, beside, across, exchange(across, "seq", 1)]
+    across = exchange(value, SEQ, 2)
+    beside = exchange(value, SEQ, 1)
+    return [value, beside, across, exchange(across, SEQ, 1)]
 
 
 def group_scatter(parts):
-    beside = exchange(jnp.stack([parts[3], parts[1]]).astype(bf16), "seq", 1)
-    far = parts[2] + beside[0].astype(f32)
-    near = parts[0] + beside[1].astype(f32)
-    return near + exchange(far.astype(bf16), "seq", 2).astype(f32)
+    sent = jnp.stack([parts[3], parts[1]]).astype(bf16)
+    return group_total(sent, jnp.stack([parts[2], parts[0]]))
+
+
+def group_total(sent, kept):
+    beside = exchange(sent, SEQ, 1)
+    far = kept[0] + beside[0].astype(f32)
+    near = kept[1] + beside[1].astype(f32)
+    return near + exchange(far.astype(bf16), SEQ, 2).astype(f32)
 
 
 def place_kernel(count):
@@ -164,20 +170,20 @@
 
 def sum_everywhere(value):
     rows = value.shape[0] // 2
-    seq = lax.axis_index("seq")
+    seq = lax.axis_index(SEQ)
     low, high = seq & 1, (seq >> 1) & 1
     halves = value.reshape(2, rows, -1)
-    mine = mine_of(halves, low, 0) + exchange(mine_of(halves, 1 - low, 0), "seq", 1)
+    mine = mine_of(halves, low, 0) + exchange(mine_of(halves, 1 - low, 0), SEQ, 1)
     halves = mine.reshape(2, rows // 2, -1)
-    mine = mine_of(halves, high, 0) + exchange(mine_of(halves, 1 - high, 0), "seq", 2)
-    for stride, radix in reversed(phases(lax.axis_size("img"))):
-        others = [mine] + [exchange(mine, "img", digit * stride) for digit in range(1, radix)]
+    mine = mine_of(halves, high, 0) + exchange(mine_of(halves, 1 - high, 0), SEQ, 2)
+    for stride, radix in reversed(phases(lax.axis_size(IMG))):
+        others = [mine] + [exchange(mine, IMG, digit * stride) for digit in range(1, radix)]
         while len(others) > 1:
             others = [others[i] + others[i + 1] for i in range(0, len(others), 2)]
         mine = others[0]
-    other = exchange(mine, "seq", 2)
+    other = exchange(mine, SEQ, 2)
     mine = jnp.where(high == 0, jnp.concatenate([mine, other]), jnp.concatenate([other, mine]))
-    other = exchange(mine, "seq", 1)
+    other = exchange(mine, SEQ, 1)
     return jnp.where(low == 0, jnp.concatenate([mine, other]), jnp.concatenate([other, mine]))
 
 
@@ -253,10 +259,9 @@
     def kernel(index_ref, x_ref, *refs):
         halves, refs = (refs[:count], refs[count : 2 * count]), refs[2 * count :]
         qb_ref, vb_ref, seg_rows, seg_cols = refs[:4]
-        w_out, wo_out, q_out, k_out, v_out, att_out, total_out = refs[4:]
+        w_out, q_out, k_out, v_out, att_out, total_out = refs[4:]
         place_in(index_ref, halves[0], w_out, (0, 2 * part), (0, 2 * part))
         place_in(index_ref, halves[1], w_out, (0, part), (2 * part, 3 * part))
-        place_in(index_ref, halves[1], wo_out, (part, 2 * part), (0, part))
         projected = jnp.dot(x_ref[...], w_out[...], preferred_element_type=f32)
         queries = (projected[:, :part] + qb_ref[...]).astype(bf16)
         for block in range(GROUP):
@@ -287,7 +292,6 @@
 
     outs = [
         ((width, 3 * part), bf16),
-        ((width, part), bf16),
         ((GROUP, rows, part), bf16),
         ((slots, part), bf16),
         ((slots, part), bf16),
@@ -445,28 +449,133 @@
     return local_call(kernel, [shape] * GROUP, [owners, left, right])
 
 
+def fold(kept, received):
+    count, rows, columns = kept.shape
+
+    def kernel(zero_ref, kept_ref, received_ref, own, *sent):
+        for digit in range(1, count):
+            sent[digit - 1][...] = (kept_ref[digit] + received_ref[digit].astype(f32)).astype(bf16)
+        own[...] = kept_ref[0] + received_ref[0].astype(f32)
+
+    outs = [((rows, columns), f32)] + [((rows, columns), bf16)] * (count - 1)
+    return local_call(kernel, outs, [jnp.zeros((1,), jnp.int32), kept, received])
+
+
+def finish(groups):
+    sizes = [len(group) for group in groups]
+    widths = [group[0].shape[1] for group in groups]
+    rows = groups[0][0].shape[0]
+
+    def kernel(zero_ref, *refs):
+        refs, out = refs[:-1], refs[-1]
+        start = column = 0
+        for size, columns in zip(sizes, widths):
+            total = refs[start][...]
+            for other in refs[start + 1 : start + size]:
+                total = total + other[...].astype(f32)
+            out[:, column : column + columns] = total.astype(bf16)
+            start, column = start + size, column + columns
+
+    inputs = [jnp.zeros((1,), jnp.int32)] + [value for group in groups for value in group]
+    return local_call(kernel, [((rows, sum(widths)), bf16)], inputs)[0]
+
+
 def scatter_pieces(pieces):
     sent, kept = pieces
-    total = kept + exchange(sent, "img", 1).astype(f32)
-    result = total[0]
-    for digit in range(1, total.shape[0]):
-        moved = exchange(total[digit].astype(bf16), "img", 2 * digit)
-        result = result + moved.astype(f32)
-    return result
+    own, *others = fold(kept, exchange(sent, IMG, 1))
+    return [own] + [exchange(other, IMG, 2 * digit) for digit, other in enumerate(others, 1)]
+
+
+def row_halves(left, right, transposed):
+    _, rows = left.shape[:2]
+    columns = right.shape[0 if transposed else 1]
+    dims = LAST if transposed else (((1,), (0,)), ((), ()))
+
+    def kernel(zero_ref, left_ref, right_ref, sent, kept):
+        for j in (3, 1, 2, 0):
+            value = lax.dot_general(left_ref[j], right_ref[...], dims, preferred_element_type=f32)
+            if j % 2:
+                sent[(3 - j) // 2] = value.astype(bf16)
+            else:
+                kept[(2 - j) // 2] = value
+
+    outs = [((2, rows, columns), bf16), ((2, rows, columns), f32)]
+    return local_call(kernel, outs, [jnp.zeros((1,), jnp.int32), left, right])
+
+
+def add_far(kept, beside):
+    def kernel(zero_ref, kept_ref, beside_ref, out):
+        out[...] = (kept_ref[0] + beside_ref[0].astype(f32)).astype(bf16)
+
+    inputs = [jnp.zeros((1,), jnp.int32), kept, beside]
+    return local_call(kernel, [(kept.shape[1:], bf16)], inputs)[0]
+
+
+def block_end(kept, beside, moved, hidden, bias, valid):
+    def kernel(zero_ref, kept_ref, beside_ref, moved_ref, hidden_ref, bias_ref, valid_ref, out):
+        branch = kept_ref[1] + beside_ref[1].astype(f32) + moved_ref[...].astype(f32)
+        value = hidden_ref[...] + branch + bias_ref[...]
+        out[...] = jnp.where(valid_ref[...] > 0, value, 0.0).astype(bf16)
+
+    inputs = [jnp.zeros((1,), jnp.int32), kept, beside, moved, hidden, bias[None]]
+    inputs.append(valid[:, None].astype(f32))
+    return local_call(kernel, [(hidden.shape, bf16)], inputs)[0]
+
+
+def output_places(index, seq_vector, parts):
+    rows, columns = parts[0].shape
+    size = columns // 2
+    per_group = len(parts) // GROUP
+
+    def kernel(index_ref, seq_ref, *refs):
+        out = refs[-1]
+        for j in range(len(parts)):
+            group, place = index_ref[j] // per_group, index_ref[j] % per_group
+            at = pl.ds(pl.multiple_of(place * rows, rows), rows)
+            out[group ^ seq_ref[0], at, :] = refs[j][:, size:]
+
+    return pl.pallas_call(
+        kernel,
+        out_shape=jax.ShapeDtypeStruct((GROUP, per_group * rows, size), bf16),
+        in_specs=[SMEM, SMEM] + [VMEM] * len(parts),
+        out_specs=VMEM,
+    )(index, seq_vector, *parts)
+
+
+def branch_halves(owners, attended, blocks):
+    _, rows, part = attended.shape
+    width = part * GROUP
+
+    def kernel(owner_ref, a_ref, *refs):
+        parts, (w_out, sent, kept) = refs[:GROUP], refs[GROUP:]
+        for k in range(GROUP):
+            w_out[:, pl.ds(pl.multiple_of(owner_ref[k] * part, part), part)] = parts[k][...]
+        for j in (3, 1, 2, 0):
+            value = jnp.dot(a_ref[j], w_out[...], preferred_element_type=f32)
+            if j % 2:
+                sent[(3 - j) // 2] = value.astype(bf16)
+            else:
+                kept[(2 - j) // 2] = value
+
+    outs = [((part, width), bf16), ((2, rows, width), bf16), ((2, rows, width), f32)]
+    return local_call(kernel, outs, [owners, attended, *blocks])
 
 
 def spread_columns(owners, parts, repeats):
     rows, total = parts[0].shape
-    size = total // repeats
+    size = total // sum(repeats)
 
     def kernel(owner_ref, *refs):
         for j in range(GROUP):
-            for r in range(repeats):
-                start = pl.multiple_of((r * GROUP + owner_ref[j]) * size, size)
-                value = refs[j][:, r * size : (r + 1) * size].astype(f32)
-                refs[GROUP][:, pl.ds(start, size)] = value
-
-    return local_call(kernel, [((rows, total * GROUP), f32)], [owners, *parts])[0]
+            column = 0
+            for out, count in zip(refs[GROUP:], repeats):
+                for r in range(count):
+                    start = pl.multiple_of((r * GROUP + owner_ref[j]) * size, size)
+                    out[:, pl.ds(start, size)] = refs[j][:, column : column + size].astype(f32)
+                    column += size
+
+    outs = [((rows, count * GROUP * size), f32) for count in repeats]
+    return local_call(kernel, outs, [owners, *parts])
 
 
 def spread_rows(owners, parts):
@@ -502,8 +611,8 @@
 ):
     shard_rows, width = tokens.shape
     group_slots = shard_rows * GROUP
-    size = lax.axis_size("img")
-    img, seq = lax.axis_index("img"), lax.axis_index("seq")
+    size = lax.axis_size(IMG)
+    img, seq = lax.axis_index(IMG), lax.axis_index(SEQ)
     held = width // size
     part = width // GROUP
     heads = HEADS // GROUP
@@ -520,7 +629,7 @@
     up_full = place(gather_relative(up_part), img).reshape(width, size * units)
     down_full = place(gather_relative(down_part), img).reshape(size * units, width)
     output_blocks = [mine_of(output_cols, seq, 0)] + [
-        exchange(mine_of(output_cols, seq ^ j, 0), "seq", j) for j in range(1, GROUP)
+        exchange(mine_of(output_cols, seq ^ j, 0), SEQ, j) for j in range(1, GROUP)
     ]
     output_full = jnp.concatenate(reorder(output_blocks, seq), axis=1)
     query_bias_part = mine_of(query_bias.reshape(GROUP, part), seq, 0)
@@ -599,7 +708,7 @@
     output_term = jnp.einsum("sc,sd->cd", attended, branch_all, preferred_element_type=f32)
     output_term = output_term.astype(bf16).reshape(part, GROUP, part)
     term_blocks = [mine_of(output_term, seq, 1)] + [
-        exchange(mine_of(output_term, seq ^ j, 1), "seq", j) for j in range(1, GROUP)
+        exchange(mine_of(output_term, seq ^ j, 1), SEQ, j) for j in range(1, GROUP)
     ]
     output_sum = to_owners(jnp.concatenate(reorder(term_blocks, seq), axis=0).astype(f32), held)
 
@@ -700,7 +809,7 @@
     second_shift,
     cotangent,
 ):
-    if up_weight.shape[1] // lax.axis_size("img") // GROUP % 128:
+    if up_weight.shape[1] // lax.axis_size(IMG) // GROUP % 128:
         return generic_device(
             tokens,
             classes,
@@ -722,8 +831,8 @@
             cotangent,
         )
     shard_rows, width = tokens.shape
-    size = lax.axis_size("img")
-    img, seq = lax.axis_index("img"), lax.axis_index("seq")
+    size = lax.axis_size(IMG)
+    img, seq = lax.axis_index(IMG), lax.axis_index(SEQ)
     held = width // size
     part = width // GROUP
     hidden_units = up_weight.shape[1]
@@ -764,41 +873,32 @@
     upstream = jnp.where(valid[:, None], cotangent.astype(f32), 0.0)
     upstream_all = jnp.concatenate(group_gather(upstream.astype(bf16)), axis=0)
 
-    input_full, output_cols, queries, keys, values, attended, totals = attention_forward(
+    columns_of = output_places(relatives, seq_vector, second_parts)
+    output_blocks = [columns_of[0]] + [exchange(columns_of[j], SEQ, j) for j in range(1, GROUP)]
+    input_full, queries, keys, values, attended, totals = attention_forward(
         relatives, normed_all, first_parts, second_parts, query_bias_part, value_bias_part, all_segments
     )
+    output_full, sent, kept = branch_halves(owners, attended, output_blocks)
     attended = attended.reshape(GROUP * shard_rows, part)
-    output_cols = output_cols.reshape(GROUP, part, part)
-    output_blocks = [mine_of(output_cols, seq, 0)] + [
-        exchange(mine_of(output_cols, seq ^ j, 0), "seq", j) for j in range(1, GROUP)
-    ]
-    output_full = jnp.concatenate(reorder(output_blocks, seq), axis=1)
-
-    def row_parts(value):
-        return [value[j * shard_rows : (j + 1) * shard_rows] for j in range(GROUP)]
-
-    branch_one = group_scatter(
-        row_parts(jnp.dot(attended, output_full, preferred_element_type=f32))
-    )
+    branch_one = group_total(sent, kept)
     hidden = embedded + branch_one + output_bias
     second_value, second_pull = jax.vjp(layer_norm, hidden, second_gain, second_shift)
     second_rows = group_gather(second_value.astype(bf16))
     up_full, second_all, active, slope = feed_forward(relatives, second_rows, up_parts, up_bias_part)
     second_all = second_all.reshape(GROUP * shard_rows, width)
-    active = active.reshape(GROUP * shard_rows, size * units)
-
-    down_sum = scatter_pieces(weight_pieces(relatives, active, upstream_all))
+    flat_active = active.reshape(GROUP * shard_rows, size * units)
+    down_sum = scatter_pieces(weight_pieces(relatives, flat_active, upstream_all))
     down_full, upper_low, upper_sums, sent, kept = feed_backward(
         relatives, upstream_all.reshape(GROUP, shard_rows, width), down_parts, slope, up_full
     )
     upper_low = upper_low.reshape(GROUP * shard_rows, size * units)
-    beside = exchange(sent, "seq", 1)
-    far = kept[0] + beside[0].astype(f32)
-    second_grad = kept[1] + beside[1].astype(f32)
-    second_grad += exchange(far.astype(bf16), "seq", 2).astype(f32)
+    second_grad = group_total(sent, kept)
     up_sum = scatter_pieces(weight_pieces(relatives, second_all, upper_low))
-    branch_two = group_scatter(row_parts(jnp.dot(active, down_full, preferred_element_type=f32)))
-    block_out = jnp.where(valid[:, None], hidden + branch_two + down_bias, 0.0).astype(bf16)
+    sent, kept = row_halves(active, down_full, False)
+    beside = exchange(sent, SEQ, 1)
+    far = add_far(kept, beside)
+    moved = exchange(far, SEQ, 2)
+    block_out = block_end(kept, beside, moved, hidden, down_bias, valid)
 
     hidden_grad, second_gain_grad, second_shift_grad = second_pull(second_grad)
     hidden_grad = hidden_grad + upstream
@@ -811,7 +911,7 @@
     projection_sums = projection_sums[0]
 
     term_blocks = group_terms(owners, attended, branch_all)
-    term_blocks = [term_blocks[0]] + [exchange(term_blocks[j], "seq", j) for j in range(1, GROUP)]
+    term_blocks = [term_blocks[0]] + [exchange(term_blocks[j], SEQ, j) for j in range(1, GROUP)]
     per_group = size // GROUP
     stacked = jnp.stack(term_blocks).reshape(size, held, part)
     pieces = [
@@ -819,20 +919,19 @@
         for j in range(size)
     ]
     output_sum = scatter_pieces((jnp.stack(pieces[1::2]), jnp.stack(pieces[0::2]).astype(f32)))
-
-    normed_grad = group_scatter(
-        row_parts(jnp.einsum("se,de->sd", projection_grad, input_full, preferred_element_type=f32)),
-    )
     input_sum = scatter_pieces(weight_pieces(relatives, normed_all, projection_grad))
+    row_grads = projection_grad.reshape(GROUP, shard_rows, 3 * part)
+    normed_grad = group_total(*row_halves(row_grads, input_full, True))
     embedded_grad, first_gain_grad, first_shift_grad = first_pull(normed_grad)
     embedded_grad = embedded_grad + hidden_grad
     table_term = jnp.einsum("st,sd->td", mixing, embedded_grad, precision=highest)
 
-    feed_shares = group_gather(jnp.stack([up_sum.astype(bf16), down_sum.astype(bf16)]))
-    up_weight_grad = spread_columns(owners, [share[0] for share in feed_shares], size)
-    down_weight_grad = spread_rows(owners, [share[1] for share in feed_shares])
-    output_weight_grad = spread_columns(owners, group_gather(output_sum.astype(bf16)), 1)
-    input_weight_grad = spread_columns(owners, group_gather(input_sum.astype(bf16)), 3)
+    up_shares = group_gather(finish([up_sum]))
+    down_shares = group_gather(finish([down_sum]))
+    last_shares = group_gather(finish([input_sum, output_sum]))
+    up_weight_grad = spread_columns(owners, up_shares, [size])[0]
+    down_weight_grad = spread_rows(owners, down_shares)
+    input_weight_grad, output_weight_grad = spread_columns(owners, last_shares, [3, 1])
 
     def spread(value, shape, axis):
         value = jnp.expand_dims(value.reshape(shape), axis)
@@ -881,41 +980,41 @@
 
 def solution(mesh):
     placed = (
-        P(("img", "seq"), None),
-        P("img"),
+        P((IMG, SEQ), None),
+        P(IMG),
         P(),
         P(),
-        P("img", None),
+        P(IMG, None),
         P(),
         P(),
-        P("img", None),
+        P(IMG, None),
         P(),
-        P("img", None),
+        P(IMG, None),
         P(),
-        P("img", None),
+        P(IMG, None),
         P(),
         P(),
         P(),
         P(),
         P(),
-        P(("img", "seq"), None),
+        P((IMG, SEQ), None),
     )
     return jax.shard_map(
         on_device,
         mesh=mesh,
         in_specs=placed,
         out_specs=(
-            P(("img", "seq"), None),
-            P(("img", "seq"), None),
+            P((IMG, SEQ), None),
+            P((IMG, SEQ), None),
             P(),
-            P("img", None),
+            P(IMG, None),
             P(),
             P(),
-            P("img", None),
+            P(IMG, None),
             P(),
-            P("img", None),
+            P(IMG, None),
             P(),
-            P("img", None),
+            P(IMG, None),
             P(),
             P(),
             P(),

time: 393 us -> 373 us (0.949)
  waiting for transfers between devices: 144 us -> 91.6 us
  Pallas kernels: 75.5 us -> 110 us
  matrix products: 11.1 us -> 2.56 us
    ppermute x87, waiting for transfers between devices: 144 us -> 91.6 us  [exchange(): return lax.ppermute(value, axis, [(i, i ^ distance) for i in range(size)])]
    pallas_call x12 -> x23, Pallas kernels: 71.7 us -> 104 us  [local_call(): pl.pallas_call(kernel, out_shape=[jax.ShapeDtypeStruct(shape, kind) for s...]
    dot_general x3 -> x0, matrix products: 7.33 us -> none  [the longest x1 4.5 us: on_device(): jnp.dot(active, down_full, preferred_element_type=f32)]
    another operation x11 -> x2, other arithmetic: 5.17 us -> 0.84 us
    unnamed x163 -> x235, local copies, waits for them, and re-layouts: 7.17 us -> 11.1 us
  transfers between devices with their start and end apart: 87 -> 87, of which waited for: 28 -> 23; matrix products, arithmetic and copies ran while one was open for 11% -> 9% of each run, Pallas kernels for 13% -> 25%
where the time goes in v1:
time: 373 us; the launch traced here: 370 us
  starting transfers between devices  120 us (32%)
  Pallas kernels  110 us (29%)
  waiting for transfers between devices  91.6 us (25%)
  other arithmetic  24.6 us (7%)
  local copies, waits for them, and re-layouts  19.4 us (5%)
    ppermute x87, starting transfers between devices, exchange(): return lax.ppermute(value, axis, [(i, i ^ distance) for i in range(size)])  120 us
    pallas_call x23, Pallas kernels, local_call(): pl.pallas_call(kernel, out_shape=[jax.ShapeDtypeStruct(shape, kind) for s...  104 us
    ppermute x87, waiting for transfers between devices, exchange(): return lax.ppermute(value, axis, [(i, i ^ distance) for i in range(size)])  91.6 us
    unnamed x235, local copies, waits for them, and re-layouts  11.1 us
  transfers between devices with their start and end apart: 87, of which 23 were waited for; matrix products, arithmetic and copies ran while one was open for 9% of the time, Pallas kernels for 25%

profile of v1, /device:TPU:1, one launch (start us, length us, event | category | flops | bytes accessed | tf_op | source)
XLA Modules:
  0.0 370.1 jit_solution(319260338289726089)
XLA Ops:
  24.2 4.7 %collective-permute-start = (bf16[152,1024]{1,0:T(8,128)(2,1)S(1)}, bf16[152,1024]{1,0:T(8,128)(2,1)S(1)}, u32[]{:S(2)}, u32[]{:S(2)}) collective-permute-start(bf16[152,1024]{1,0:T(8,128)(2,1)S(1)} %add_convert_fusion.4), channel_id=1, source_target_pairs={{0,1},{1,0},{2,3},{3,2},{4,5},{5,4},{6,7},{7,6},{8,9},{9,8},{10,11... | collective-permute-start | bytes 933896 | tf_op jit(solution)/shard_map/ppermute | solution.py:81
  40.1 4.8 %collective-permute-start.17 = (bf16[256,256]{1,0:T(8,128)(2,1)S(1)}, bf16[256,256]{1,0:T(8,128)(2,1)S(1)}, u32[]{:S(2)}, u32[]{:S(2)}) collective-permute-start(bf16[256,256]{1,0:T(8,128)(2,1)S(1)} %get-tuple-element.163), channel_id=1, source_target_pairs={{0,1},{1,0},{2,3},{3,2},{4,5},{5,4},{6,7},{7,6},{8,9},{9,8},{10,11... | collective-permute-start | bytes 393224 | tf_op jit(solution)/shard_map/ppermute | solution.py:81
  48.5 12.4 %shard_map.298 = (bf16[1024,768]{1,0:T(8,128)(2,1)}, bf16[4,152,256]{2,1,0:T(8,128)(2,1)}, bf16[608,256]{1,0:T(8,128)(2,1)}, bf16[608,256]{1,0:T(8,128)(2,1)}, b...) custom-call(s32[8]{0:T(128)} %iota_xor_fusion.1.index_ref, bf16[608,1024]{1,0:T(8,128)(2,1)} %pad_maximum_fusion.x_ref.left_ref, ...), custom_call_target="tpu_custom_call" | custom-call | tf_op jit(solution)/shard_map/pallas_call | solution.py:206
  61.7 2.8 shard_map.300
  85.9 10.3 %collective-permute-start.32 = (bf16[152,1024]{1,0:T(8,128)(2,1)S(1)}, bf16[152,1024]{1,0:T(8,128)(2,1)S(1)}, u32[]{:S(2)}, u32[]{:S(2)}) collective-permute-start(bf16[152,1024]{1,0:T(8,128)(2,1)S(1)} %fusion.3), channel_id=1, source_target_pairs={{0,1},{1,0},{2,3},{3,2},{4,5},{5,4},{6,7},{7,6},{8,9},{9,8},{10,11... | collective-permute-start | bytes 933896 | tf_op jit(solution)/shard_map/ppermute | solution.py:81
  99.5 15.7 %collective-permute-done.38.refs_4_ = bf16[128,1024]{1,0:T(8,128)(2,1)S(1)} collective-permute-done((bf16[128,1024]{1,0:T(8,128)(2,1)S(1)}, bf16[128,1024]{1,0:T(8,128)(2,1)S(1)}, u32[]{:S(2)}, u32[]{:S(2)}) %collective-permute-start.38) | collective-permute-done | bytes 262176 | tf_op jit(solution)/shard_map/ppermute | solution.py:81
  116.3 3.9 %collective-permute-start.34 = (bf16[152,1024]{1,0:T(8,128)(2,1)S(1)}, bf16[152,1024]{1,0:T(8,128)(2,1)S(1)}, u32[]{:S(2)}, u32[]{:S(2)}) collective-permute-start(bf16[152,1024]{1,0:T(8,128)(2,1)S(1)} %collective-permute-done.33), channel_id=1, source_target_pairs={{0,1},{1,0},{2,3},{3,2},{4,5},{5,4},{6,7},{7,6},{8,9},{9,8},{10,11... | collective-permute-start | bytes 933896 | tf_op jit(solution)/shard_map/ppermute | solution.py:81
  121.8 3.8 %collective-permute-start.24 = (bf16[152,1024]{1,0:T(8,128)(2,1)S(1)}, bf16[152,1024]{1,0:T(8,128)(2,1)S(1)}, u32[]{:S(2)}, u32[]{:S(2)}) collective-permute-start(bf16[152,1024]{1,0:T(8,128)(2,1)S(1)} %collective-permute-done.23.refs_2_), channel_id=1, source_target_pairs={{0,1},{1,0},{2,3},{3,2},{4,5},{5,4},{6,7},{7,6},{8,9},{9,8},{10,11... | collective-permute-start | bytes 933896 | tf_op jit(solution)/shard_map/ppermute | solution.py:81
  128.9 4.4 %collective-permute-done.31.refs_11_ = bf16[128,1024]{1,0:T(8,128)(2,1)S(1)} collective-permute-done((bf16[128,1024]{1,0:T(8,128)(2,1)S(1)}, bf16[128,1024]{1,0:T(8,128)(2,1)S(1)}, u32[]{:S(2)}, u32[]{:S(2)}) %collective-permute-start.31) | collective-permute-done | bytes 262176 | tf_op jit(solution)/shard_map/ppermute | solution.py:81
  139.3 8.8 %shard_map.302 = (bf16[1024,1024]{1,0:T(8,128)(2,1)}, bf16[4,152,1024]{2,1,0:T(8,128)(2,1)}, bf16[4,152,1024]{2,1,0:T(8,128)(2,1)}, f32[4,152,1024]{2,1,0:T(8,128)}) custom-call(s32[8]{0:T(128)} %iota_xor_fusion.1.index_ref, bf16[152,1024]{1,0:T(8,128)(2,1)} %copy-done.8, bf16[152,1024]{1,0:T(8,128)(2,1)} %copy-done.34, bf16[152,1024]{1,0:T(8,128)(2,1)} %copy-done.33, ...), custom_call_target="tpu_custom_call" | custom-call | tf_op jit(solution)/shard_map/pallas_call | solution.py:206
  150.2 5.6 %collective-permute-done.41.refs_7_ = bf16[128,1024]{1,0:T(8,128)(2,1)S(1)} collective-permute-done((bf16[128,1024]{1,0:T(8,128)(2,1)S(1)}, bf16[128,1024]{1,0:T(8,128)(2,1)S(1)}, u32[]{:S(2)}, u32[]{:S(2)}) %collective-permute-start.41) | collective-permute-done | bytes 262176 | tf_op jit(solution)/shard_map/ppermute | solution.py:81
  156.5 10.2 %shard_map.303 = (bf16[1024,1024]{1,0:T(8,128)(2,1)}, bf16[4,152,1024]{2,1,0:T(8,128)(2,1)}, f32[1,1024]{1,0:T(1,128)}, bf16[2,152,1024]{2,1,0:T(8,128)(2,1)}, f32[2,152,1024]{2,1,0:T(8,128)}) custom-call(s32[8]{0:T(128)} %iota_xor_fusion.1.index_ref, bf16[4,152,1024]{2,1,0:T(8,128)(2,1)} %bitcast.92, bf16[128,1024]{1,0:T(8,128)(2,1)} %get-tuple-element.79.refs_0_, ...), custom_call_target="tpu_custom_call" | custom-call | tf_op jit(solution)/shard_map/pallas_call | solution.py:206
  171.4 8.3 %collective-permute-done.45 = bf16[152,1024]{1,0:T(8,128)(2,1)S(1)} collective-permute-done((bf16[152,1024]{1,0:T(8,128)(2,1)S(1)}, bf16[152,1024]{1,0:T(8,128)(2,1)S(1)}, u32[]{:S(2)}, u32[]{:S(2)}) %collective-permute-start.45) | collective-permute-done | bytes 311328 | tf_op jit(solution)/shard_map/ppermute | solution.py:81
  182.6 4.9 %shard_map.315 = (bf16[4,128,1024]{2,1,0:T(8,128)(2,1)}, f32[4,128,1024]{2,1,0:T(8,128)}) custom-call(s32[8]{0:T(128)} %iota_xor_fusion.1.index_ref, bf16[608,1024]{1,0:T(8,128)(2,1)} %bitcast.97, bf16[608,1024]{1,0:T(8,128)(2,1)} %bitcast.98), custom_call_target="tpu_custom_call" | custom-call | tf_op jit(solution)/shard_map/pallas_call | solution.py:206
  188.7 4.9 %shard_map.319 = (bf16[4,128,1024]{2,1,0:T(8,128)(2,1)}, f32[4,128,1024]{2,1,0:T(8,128)}) custom-call(s32[8]{0:T(128)} %iota_xor_fusion.1.index_ref, bf16[608,1024]{1,0:T(8,128)(2,1)} %bitcast.93, bf16[608,1024]{1,0:T(8,128)(2,1)} %pad_maximum_fusion.1.right_ref), custom_call_target="tpu_custom_call" | custom-call | tf_op jit(solution)/shard_map/pallas_call | solution.py:206
  198.9 13.5 %shard_map.307 = (bf16[608,768]{1,0:T(8,128)(2,1)}, f32[1,768]{1,0:T(1,128)}) custom-call(s32[1]{0:T(128)} %constant.196.clone.1.zero_ref, bf16[4,152,256]{2,1,0:T(8,128)(2,1)} %get-tuple-element.85.q_ref, bf16[608,256]{1,0:T(8,128)(2,1)} %get-tuple-element.86.k_ref, bf16[608,256]{1,0:T(8,128)(2,1)} %get-tuple-element.87.v_ref, ...), custom_call_target="tpu_custom_call" | custom-call | tf_op jit(solution)/shard_map/pallas_call | solution.py:206
  212.4 4.9 %shard_map.308 = (bf16[2,152,1024]{2,1,0:T(8,128)(2,1)}, f32[2,152,1024]{2,1,0:T(8,128)}) custom-call(s32[1]{0:T(128)} %constant.196.clone.1.zero_ref, bf16[4,152,768]{2,1,0:T(8,128)(2,1)} %bitcast.94, bf16[1024,768]{1,0:T(8,128)(2,1)} %get-tuple-element.93.right_ref), custom_call_target="tpu_custom_call" | custom-call | tf_op jit(solution)/shard_map/pallas_call | solution.py:206
  217.7 4.6 %shard_map.304 = (bf16[2,152,1024]{2,1,0:T(8,128)(2,1)}, f32[2,152,1024]{2,1,0:T(8,128)}) custom-call(s32[1]{0:T(128)} %constant.196.clone.1.zero_ref, bf16[4,152,1024]{2,1,0:T(8,128)(2,1)} %get-tuple-element.78.left_ref, bf16[1024,1024]{1,0:T(8,128)(2,1)} %get-tuple-element.82.right_ref), custom_call_target="tpu_custom_call" | custom-call | tf_op jit(solution)/shard_map/pallas_call | solution.py:206
  223.8 3.0 shard_map.316
  226.8 3.7 collective-permute-start.74
  230.5 3.0 collective-permute-done.80.received_ref
  234.4 3.0 shard_map.320
  237.5 4.3 %shard_map.309 = (bf16[4,128,768]{2,1,0:T(8,128)(2,1)}, f32[4,128,768]{2,1,0:T(8,128)}) custom-call(s32[8]{0:T(128)} %iota_xor_fusion.1.index_ref, bf16[608,1024]{1,0:T(8,128)(2,1)} %pad_maximum_fusion.x_ref.left_ref, bf16[608,768]{1,0:T(8,128)(2,1)} %get-tuple-element.92.right_ref), custom_call_target="tpu_custom_call" | custom-call | tf_op jit(solution)/shard_map/pallas_call | solution.py:206
  245.5 2.7 shard_map.311
  256.8 4.8 %collective-permute-start.75 = (bf16[128,1024]{1,0:T(8,128)(2,1)}, bf16[128,1024]{1,0:T(8,128)(2,1)S(1)}, u32[]{:S(2)}, u32[]{:S(2)}) collective-permute-start(bf16[128,1024]{1,0:T(8,128)(2,1)} %get-tuple-element.120), channel_id=1, source_target_pairs={{0,16},{4,20},{8,24},{12,28},{16,0},{20,4},{24,8},{28,12},{1,17},{... | collective-permute-start | bytes 786440 | tf_op jit(solution)/shard_map/ppermute | solution.py:81
  266.9 12.9 %collective-permute-done.75.refs_2_ = bf16[128,1024]{1,0:T(8,128)(2,1)S(1)} collective-permute-done((bf16[128,1024]{1,0:T(8,128)(2,1)}, bf16[128,1024]{1,0:T(8,128)(2,1)S(1)}, u32[]{:S(2)}, u32[]{:S(2)}) %collective-permute-start.75) | collective-permute-done | bytes 262176 | tf_op jit(solution)/shard_map/ppermute | solution.py:81
  286.9 15.3 %collective-permute-done.82.refs_2_ = bf16[128,1024]{1,0:T(8,128)(2,1)S(1)} collective-permute-done((bf16[128,1024]{1,0:T(8,128)(2,1)}, bf16[128,1024]{1,0:T(8,128)(2,1)S(1)}, u32[]{:S(2)}, u32[]{:S(2)}) %collective-permute-start.82) | collective-permute-done | bytes 262176 | tf_op jit(solution)/shard_map/ppermute | solution.py:81
  310.4 5.1 %collective-permute-start.67 = (bf16[128,256]{1,0:T(8,128)(2,1)}, bf16[128,256]{1,0:T(8,128)(2,1)S(1)}, u32[]{:S(2)}, u32[]{:S(2)}) collective-permute-start(bf16[128,256]{1,0:T(8,128)(2,1)} %get-tuple-element.109), channel_id=1, source_target_pairs={{0,8},{4,12},{8,0},{12,4},{16,24},{20,28},{24,16},{28,20},{1,9},{5... | collective-permute-start | bytes 196616 | tf_op jit(solution)/shard_map/ppermute | solution.py:81
  318.0 3.6 collective-permute-done.85.refs_2_
  334.4 7.6 %collective-permute-done.60.refs_1_ = bf16[128,768]{1,0:T(8,128)(2,1)S(1)} collective-permute-done((bf16[128,768]{1,0:T(8,128)(2,1)}, bf16[128,768]{1,0:T(8,128)(2,1)S(1)}, u32[]{:S(2)}, u32[]{:S(2)}) %collective-permute-start.60) | collective-permute-done | bytes 196640 | tf_op jit(solution)/shard_map/ppermute | solution.py:81
  342.5 5.8 %collective-permute-start.79 = (bf16[128,1024]{1,0:T(8,128)(2,1)S(1)}, bf16[128,1024]{1,0:T(8,128)(2,1)S(1)}, u32[]{:S(2)}, u32[]{:S(2)}) collective-permute-start(bf16[128,1024]{1,0:T(8,128)(2,1)S(1)} %collective-permute-done.78.refs_2_), channel_id=1, source_target_pairs={{0,1},{1,0},{2,3},{3,2},{4,5},{5,4},{6,7},{7,6},{8,9},{9,8},{10,11... | collective-permute-start | bytes 786440 | tf_op jit(solution)/shard_map/ppermute | solution.py:81
  356.6 2.8 shard_map.318
  (483 shorter events, 161.7 us)
Async XLA Ops:
  2.4 17.6 %collective-permute-start.10 = (bf16[128,512]{1,0:T(8,128)(2,1)}, bf16[128,512]{1,0:T(8,128)(2,1)S(1)}, u32[]{:S(2)}, u32[]{:S(2)}) collective-permute-start(bf16[128,512]{1,0:T(8,128)(2,1)} %get-tuple-element.73.refs_8_.refs_0_), channel_id=1, source_target_pairs={{0,4},{4,0},{8,12},{12,8},{16,20},{20,16},{24,28},{28,24},{1,5},{5... | collective-permute-start | bytes 393224 | tf_op jit(solution)/shard_map/ppermute | solution.py:81
  24.2 20.7 %collective-permute-start = (bf16[152,1024]{1,0:T(8,128)(2,1)S(1)}, bf16[152,1024]{1,0:T(8,128)(2,1)S(1)}, u32[]{:S(2)}, u32[]{:S(2)}) collective-permute-start(bf16[152,1024]{1,0:T(8,128)(2,1)S(1)} %add_convert_fusion.4), channel_id=1, source_target_pairs={{0,1},{1,0},{2,3},{3,2},{4,5},{5,4},{6,7},{7,6},{8,9},{9,8},{10,11... | collective-permute-start | bytes 933896 | tf_op jit(solution)/shard_map/ppermute | solution.py:81
  29.0 16.2 %collective-permute-start.2 = (bf16[152,1024]{1,0:T(8,128)(2,1)S(1)}, bf16[152,1024]{1,0:T(8,128)(2,1)S(1)}, u32[]{:S(2)}, u32[]{:S(2)}) collective-permute-start(bf16[152,1024]{1,0:T(8,128)(2,1)S(1)} %collective-permute-done.1), channel_id=1, source_target_pairs={{0,1},{1,0},{2,3},{3,2},{4,5},{5,4},{6,7},{7,6},{8,9},{9,8},{10,11... | collective-permute-start | bytes 933896 | tf_op jit(solution)/shard_map/ppermute | solution.py:81
  40.1 20.8 %collective-permute-start.17 = (bf16[256,256]{1,0:T(8,128)(2,1)S(1)}, bf16[256,256]{1,0:T(8,128)(2,1)S(1)}, u32[]{:S(2)}, u32[]{:S(2)}) collective-permute-start(bf16[256,256]{1,0:T(8,128)(2,1)S(1)} %get-tuple-element.163), channel_id=1, source_target_pairs={{0,1},{1,0},{2,3},{3,2},{4,5},{5,4},{6,7},{7,6},{8,9},{9,8},{10,11... | collective-permute-start | bytes 393224 | tf_op jit(solution)/shard_map/ppermute | solution.py:81
  75.3 21.0 %collective-permute-start.30 = (bf16[128,1024]{1,0:T(8,128)(2,1)}, bf16[128,1024]{1,0:T(8,128)(2,1)S(1)}, u32[]{:S(2)}, u32[]{:S(2)}) collective-permute-start(bf16[128,1024]{1,0:T(8,128)(2,1)} %get-tuple-element.77.refs_4_), channel_id=1, source_target_pairs={{0,24},{4,28},{8,16},{12,20},{16,8},{20,12},{24,0},{28,4},{1,25},{... | collective-permute-start | bytes 786440 | tf_op jit(solution)/shard_map/ppermute | solution.py:81
  78.0 20.5 %collective-permute-start.36 = (bf16[128,1024]{1,0:T(8,128)(2,1)}, bf16[128,1024]{1,0:T(8,128)(2,1)S(1)}, u32[]{:S(2)}, u32[]{:S(2)}) collective-permute-start(bf16[128,1024]{1,0:T(8,128)(2,1)} %get-tuple-element.79.refs_0_), channel_id=1, source_target_pairs={{0,8},{4,12},{8,0},{12,4},{16,24},{20,28},{24,16},{28,20},{1,9},{5... | collective-permute-start | bytes 786440 | tf_op jit(solution)/shard_map/ppermute | solution.py:81
  81.1 34.1 %collective-permute-start.38 = (bf16[128,1024]{1,0:T(8,128)(2,1)S(1)}, bf16[128,1024]{1,0:T(8,128)(2,1)S(1)}, u32[]{:S(2)}, u32[]{:S(2)}) collective-permute-start(bf16[128,1024]{1,0:T(8,128)(2,1)S(1)} %copy-done.36), channel_id=1, source_target_pairs={{0,16},{4,20},{8,24},{12,28},{16,0},{20,4},{24,8},{28,12},{1,17},{... | collective-permute-start | bytes 786440 | tf_op jit(solution)/shard_map/ppermute | solution.py:81
  84.8 31.5 %collective-permute-start.33 = (bf16[152,1024]{1,0:T(8,128)(2,1)S(1)}, bf16[152,1024]{1,0:T(8,128)(2,1)S(1)}, u32[]{:S(2)}, u32[]{:S(2)}) collective-permute-start(bf16[152,1024]{1,0:T(8,128)(2,1)S(1)} %fusion.3), channel_id=1, source_target_pairs={{0,2},{1,3},{2,0},{3,1},{4,6},{5,7},{6,4},{7,5},{8,10},{9,11},{10,... | collective-permute-start | bytes 933896 | tf_op jit(solution)/shard_map/ppermute | solution.py:81
  85.9 34.4 %collective-permute-start.32 = (bf16[152,1024]{1,0:T(8,128)(2,1)S(1)}, bf16[152,1024]{1,0:T(8,128)(2,1)S(1)}, u32[]{:S(2)}, u32[]{:S(2)}) collective-permute-start(bf16[152,1024]{1,0:T(8,128)(2,1)S(1)} %fusion.3), channel_id=1, source_target_pairs={{0,1},{1,0},{2,3},{3,2},{4,5},{5,4},{6,7},{7,6},{8,9},{9,8},{10,11... | collective-permute-start | bytes 933896 | tf_op jit(solution)/shard_map/ppermute | solution.py:81
  96.3 24.0 %collective-permute-start.40 = (bf16[128,1024]{1,0:T(8,128)(2,1)S(1)}, bf16[128,1024]{1,0:T(8,128)(2,1)S(1)}, u32[]{:S(2)}, u32[]{:S(2)}) collective-permute-start(bf16[128,1024]{1,0:T(8,128)(2,1)S(1)} %copy-done.36), channel_id=1, source_target_pairs={{0,24},{4,28},{8,16},{12,20},{16,8},{20,12},{24,0},{28,4},{1,25},{... | collective-permute-start | bytes 786440 | tf_op jit(solution)/shard_map/ppermute | solution.py:81
  98.5 23.0 %collective-permute-start.27 = (bf16[128,1024]{1,0:T(8,128)(2,1)S(1)}, bf16[128,1024]{1,0:T(8,128)(2,1)S(1)}, u32[]{:S(2)}, u32[]{:S(2)}) collective-permute-start(bf16[128,1024]{1,0:T(8,128)(2,1)S(1)} %collective-permute-done.26.refs_6_), channel_id=1, source_target_pairs={{0,4},{4,0},{8,12},{12,8},{16,20},{20,16},{24,28},{28,24},{1,5},{5... | collective-permute-start | bytes 786440 | tf_op jit(solution)/shard_map/ppermute | solution.py:81
  116.3 18.3 %collective-permute-start.34 = (bf16[152,1024]{1,0:T(8,128)(2,1)S(1)}, bf16[152,1024]{1,0:T(8,128)(2,1)S(1)}, u32[]{:S(2)}, u32[]{:S(2)}) collective-permute-start(bf16[152,1024]{1,0:T(8,128)(2,1)S(1)} %collective-permute-done.33), channel_id=1, source_target_pairs={{0,1},{1,0},{2,3},{3,2},{4,5},{5,4},{6,7},{7,6},{8,9},{9,8},{10,11... | collective-permute-start | bytes 933896 | tf_op jit(solution)/shard_map/ppermute | solution.py:81
  121.8 16.7 %collective-permute-start.24 = (bf16[152,1024]{1,0:T(8,128)(2,1)S(1)}, bf16[152,1024]{1,0:T(8,128)(2,1)S(1)}, u32[]{:S(2)}, u32[]{:S(2)}) collective-permute-start(bf16[152,1024]{1,0:T(8,128)(2,1)S(1)} %collective-permute-done.23.refs_2_), channel_id=1, source_target_pairs={{0,1},{1,0},{2,3},{3,2},{4,5},{5,4},{6,7},{7,6},{8,9},{9,8},{10,11... | collective-permute-start | bytes 933896 | tf_op jit(solution)/shard_map/ppermute | solution.py:81
  127.8 20.4 %collective-permute-start.35 = (bf16[128,1024]{1,0:T(8,128)(2,1)S(1)}, bf16[128,1024]{1,0:T(8,128)(2,1)S(1)}, u32[]{:S(2)}, u32[]{:S(2)}) collective-permute-start(bf16[128,1024]{1,0:T(8,128)(2,1)S(1)} %copy-done.36), channel_id=1, source_target_pairs={{0,4},{4,0},{8,12},{12,8},{16,20},{20,16},{24,28},{28,24},{1,5},{5... | collective-permute-start | bytes 786440 | tf_op jit(solution)/shard_map/ppermute | solution.py:81
  134.8 21.0 %collective-permute-start.41 = (bf16[128,1024]{1,0:T(8,128)(2,1)S(1)}, bf16[128,1024]{1,0:T(8,128)(2,1)S(1)}, u32[]{:S(2)}, u32[]{:S(2)}) collective-permute-start(bf16[128,1024]{1,0:T(8,128)(2,1)S(1)} %collective-permute-done.40.refs_6_), channel_id=1, source_target_pairs={{0,4},{4,0},{8,12},{12,8},{16,20},{20,16},{24,28},{28,24},{1,5},{5... | collective-permute-start | bytes 786440 | tf_op jit(solution)/shard_map/ppermute | solution.py:81
  187.5 36.4 %collective-permute-start.73 = (bf16[4,128,1024]{2,1,0:T(8,128)(2,1)}, bf16[4,128,1024]{2,1,0:T(8,128)(2,1)}, u32[]{:S(2)}, u32[]{:S(2)}) collective-permute-start(bf16[4,128,1024]{2,1,0:T(8,128)(2,1)} %get-tuple-element.117), channel_id=1, source_target_pairs={{0,4},{4,0},{8,12},{12,8},{16,20},{20,16},{24,28},{28,24},{1,5},{5... | collective-permute-start | bytes 3145736 | tf_op jit(solution)/shard_map/ppermute | solution.py:81
  193.6 39.9 %collective-permute-start.80 = (bf16[4,128,1024]{2,1,0:T(8,128)(2,1)}, bf16[4,128,1024]{2,1,0:T(8,128)(2,1)S(1)}, u32[]{:S(2)}, u32[]{:S(2)}) collective-permute-start(bf16[4,128,1024]{2,1,0:T(8,128)(2,1)} %get-tuple-element.123), channel_id=1, source_target_pairs={{0,4},{4,0},{8,12},{12,8},{16,20},{20,16},{24,28},{28,24},{1,5},{5... | collective-permute-start | bytes 3145736 | tf_op jit(solution)/shard_map/ppermute | solution.py:81
  217.3 24.5 %collective-permute-start.49 = (bf16[2,152,1024]{2,1,0:T(8,128)(2,1)}, bf16[2,152,1024]{2,1,0:T(8,128)(2,1)}, u32[]{:S(2)}, u32[]{:S(2)}) collective-permute-start(bf16[2,152,1024]{2,1,0:T(8,128)(2,1)} %get-tuple-element.95), channel_id=1, source_target_pairs={{0,1},{1,0},{2,3},{3,2},{4,5},{5,4},{6,7},{7,6},{8,9},{9,8},{10,11... | collective-permute-start | bytes 1867784 | tf_op jit(solution)/shard_map/ppermute | solution.py:81
  222.3 41.1 %collective-permute-start.42 = (bf16[2,152,1024]{2,1,0:T(8,128)(2,1)}, bf16[2,152,1024]{2,1,0:T(8,128)(2,1)S(1)}, u32[]{:S(2)}, u32[]{:S(2)}) collective-permute-start(bf16[2,152,1024]{2,1,0:T(8,128)(2,1)} %get-tuple-element.84), channel_id=1, source_target_pairs={{0,1},{1,0},{2,3},{3,2},{4,5},{5,4},{6,7},{7,6},{8,9},{9,8},{10,11... | collective-permute-start | bytes 1867784 | tf_op jit(solution)/shard_map/ppermute | solution.py:81
  226.8 38.7 %collective-permute-start.74 = (bf16[128,1024]{1,0:T(8,128)(2,1)}, bf16[128,1024]{1,0:T(8,128)(2,1)}, u32[]{:S(2)}, u32[]{:S(2)}) collective-permute-start(bf16[128,1024]{1,0:T(8,128)(2,1)} %get-tuple-element.119), channel_id=1, source_target_pairs={{0,8},{4,12},{8,0},{12,4},{16,24},{20,28},{24,16},{28,20},{1,9},{5... | collective-permute-start | bytes 786440 | tf_op jit(solution)/shard_map/ppermute | solution.py:81
  256.8 22.9 %collective-permute-start.75 = (bf16[128,1024]{1,0:T(8,128)(2,1)}, bf16[128,1024]{1,0:T(8,128)(2,1)S(1)}, u32[]{:S(2)}, u32[]{:S(2)}) collective-permute-start(bf16[128,1024]{1,0:T(8,128)(2,1)} %get-tuple-element.120), channel_id=1, source_target_pairs={{0,16},{4,20},{8,24},{12,28},{16,0},{20,4},{24,8},{28,12},{1,17},{... | collective-permute-start | bytes 786440 | tf_op jit(solution)/shard_map/ppermute | solution.py:81
  261.6 19.2 %collective-permute-start.76 = (bf16[128,1024]{1,0:T(8,128)(2,1)}, bf16[128,1024]{1,0:T(8,128)(2,1)S(1)}, u32[]{:S(2)}, u32[]{:S(2)}) collective-permute-start(bf16[128,1024]{1,0:T(8,128)(2,1)} %get-tuple-element.121), channel_id=1, source_target_pairs={{0,24},{4,28},{8,16},{12,20},{16,8},{20,12},{24,0},{28,4},{1,25},{... | collective-permute-start | bytes 786440 | tf_op jit(solution)/shard_map/ppermute | solution.py:81
  263.4 18.0 %collective-permute-start.81 = (bf16[128,1024]{1,0:T(8,128)(2,1)S(1)}, bf16[128,1024]{1,0:T(8,128)(2,1)S(1)}, u32[]{:S(2)}, u32[]{:S(2)}) collective-permute-start(bf16[128,1024]{1,0:T(8,128)(2,1)S(1)} %copy-done.113), channel_id=1, source_target_pairs={{0,8},{4,12},{8,0},{12,4},{16,24},{20,28},{24,16},{28,20},{1,9},{5... | collective-permute-start | bytes 786440 | tf_op jit(solution)/shard_map/ppermute | solution.py:81
  264.2 58.4 %collective-permute-start.59 = (bf16[4,128,768]{2,1,0:T(8,128)(2,1)}, bf16[4,128,768]{2,1,0:T(8,128)(2,1)S(1)}, u32[]{:S(2)}, u32[]{:S(2)}) collective-permute-start(bf16[4,128,768]{2,1,0:T(8,128)(2,1)} %get-tuple-element.99), channel_id=1, source_target_pairs={{0,4},{4,0},{8,12},{12,8},{16,20},{20,16},{24,28},{28,24},{1,5},{5... | collective-permute-start | bytes 2359304 | tf_op jit(solution)/shard_map/ppermute | solution.py:81
  265.5 36.8 %collective-permute-start.82 = (bf16[128,1024]{1,0:T(8,128)(2,1)}, bf16[128,1024]{1,0:T(8,128)(2,1)S(1)}, u32[]{:S(2)}, u32[]{:S(2)}) collective-permute-start(bf16[128,1024]{1,0:T(8,128)(2,1)} %get-tuple-element.126), channel_id=1, source_target_pairs={{0,16},{4,20},{8,24},{12,28},{16,0},{20,4},{24,8},{28,12},{1,17},{... | collective-permute-start | bytes 786440 | tf_op jit(solution)/shard_map/ppermute | solution.py:81
  279.8 22.8 %collective-permute-start.83 = (bf16[128,1024]{1,0:T(8,128)(2,1)}, bf16[128,1024]{1,0:T(8,128)(2,1)}, u32[]{:S(2)}, u32[]{:S(2)}) collective-permute-start(bf16[128,1024]{1,0:T(8,128)(2,1)} %get-tuple-element.127), channel_id=1, source_target_pairs={{0,24},{4,28},{8,16},{12,20},{16,8},{20,12},{24,0},{28,4},{1,25},{... | collective-permute-start | bytes 786440 | tf_op jit(solution)/shard_map/ppermute | solution.py:81
  280.8 25.0 %collective-permute-start.52 = (f32[16,1024]{1,0:T(8,128)S(1)}, f32[16,1024]{1,0:T(8,128)S(1)}, u32[]{:S(2)}, u32[]{:S(2)}) collective-permute-start(f32[16,1024]{1,0:T(8,128)S(1)} %dynamic-slice_bitcast_fusion.1), channel_id=1, source_target_pairs={{0,2},{1,3},{2,0},{3,1},{4,6},{5,7},{6,4},{7,5},{8,10},{9,11},{10,... | collective-permute-start | bytes 196616 | tf_op jit(solution)/shard_map/ppermute | solution.py:81
  281.5 24.7 %collective-permute-start.66 = (bf16[4,128,256]{2,1,0:T(8,128)(2,1)S(1)}, bf16[4,128,256]{2,1,0:T(8,128)(2,1)S(1)}, u32[]{:S(2)}, u32[]{:S(2)}) collective-permute-start(bf16[4,128,256]{2,1,0:T(8,128)(2,1)S(1)} %pad_maximum_fusion.4), channel_id=1, source_target_pairs={{0,4},{4,0},{8,12},{12,8},{16,20},{20,16},{24,28},{28,24},{1,5},{5... | collective-permute-start | bytes 786440 | tf_op jit(solution)/shard_map/ppermute | solution.py:81
  326.1 25.3 %collective-permute-start.77 = (bf16[128,1024]{1,0:T(8,128)(2,1)S(1)}, bf16[128,1024]{1,0:T(8,128)(2,1)S(1)}, u32[]{:S(2)}, u32[]{:S(2)}) collective-permute-start(bf16[128,1024]{1,0:T(8,128)(2,1)S(1)} %copy-done.11), channel_id=1, source_target_pairs={{0,1},{1,0},{2,3},{3,2},{4,5},{5,4},{6,7},{7,6},{8,9},{9,8},{10,11... | collective-permute-start | bytes 786440 | tf_op jit(solution)/shard_map/ppermute | solution.py:81
  331.8 16.6 %collective-permute-start.62 = (bf16[128,768]{1,0:T(8,128)(2,1)}, bf16[128,768]{1,0:T(8,128)(2,1)S(1)}, u32[]{:S(2)}, u32[]{:S(2)}) collective-permute-start(bf16[128,768]{1,0:T(8,128)(2,1)} %get-tuple-element.103), channel_id=1, source_target_pairs={{0,24},{4,28},{8,16},{12,20},{16,8},{20,12},{24,0},{28,4},{1,25},{... | collective-permute-start | bytes 589832 | tf_op jit(solution)/shard_map/ppermute | solution.py:81
  334.0 17.1 %collective-permute-start.57 = (f32[16,1024]{1,0:T(8,128)S(1)}, f32[16,1024]{1,0:T(8,128)S(1)}, u32[]{:S(2)}, u32[]{:S(2)}) collective-permute-start(f32[16,1024]{1,0:T(8,128)S(1)} %add_add_fusion.4), channel_id=1, source_target_pairs={{0,2},{1,3},{2,0},{3,1},{4,6},{5,7},{6,4},{7,5},{8,10},{9,11},{10,... | collective-permute-start | bytes 196616 | tf_op jit(solution)/shard_map/ppermute | solution.py:81
  341.9 17.5 %collective-permute-start.84 = (bf16[128,1024]{1,0:T(8,128)(2,1)S(1)}, bf16[128,1024]{1,0:T(8,128)(2,1)S(1)}, u32[]{:S(2)}, u32[]{:S(2)}) collective-permute-start(bf16[128,1024]{1,0:T(8,128)(2,1)S(1)} %copy-done.12), channel_id=1, source_target_pairs={{0,1},{1,0},{2,3},{3,2},{4,5},{5,4},{6,7},{7,6},{8,9},{9,8},{10,11... | collective-permute-start | bytes 786440 | tf_op jit(solution)/shard_map/ppermute | solution.py:81
  (170 other events, 1861.6 us)

commit v2 on v1

--- a/solution.py
+++ b/solution.py
@@ -260,8 +260,8 @@
         halves, refs = (refs[:count], refs[count : 2 * count]), refs[2 * count :]
         qb_ref, vb_ref, seg_rows, seg_cols = refs[:4]
         w_out, q_out, k_out, v_out, att_out, total_out = refs[4:]
-        place_in(index_ref, halves[0], w_out, (0, 2 * part), (0, 2 * part))
-        place_in(index_ref, halves[1], w_out, (0, part), (2 * part, 3 * part))
+        place_in(index_ref, halves[0], w_out, (0, part), (0, part))
+        place_in(index_ref, halves[1], w_out, (0, 2 * part), (part, 3 * part))
         projected = jnp.dot(x_ref[...], w_out[...], preferred_element_type=f32)
         queries = (projected[:, :part] + qb_ref[...]).astype(bf16)
         for block in range(GROUP):
@@ -841,8 +841,8 @@
     owners = seq ^ jnp.arange(GROUP, dtype=jnp.int32)
     seq_vector = seq[None].astype(jnp.int32)
 
-    blocks = [(0, 1, t * width, 0, t * part, part) for t in range(2)]
-    blocks += [(0, 1, 2 * width, 1, 0, part), (1, 1, 0, 1, part, part)]
+    blocks = [(0, 1, t * width, 1, (t - 1) * part, part) for t in (1, 2)]
+    blocks += [(0, 1, 0, 0, 0, part), (1, 1, 0, 0, part, part)]
     first_part, second_part = pick(
         [input_weight, output_weight], blocks, [(held, 2 * part)] * 2, seq_vector
     )
@@ -873,7 +873,7 @@
     upstream = jnp.where(valid[:, None], cotangent.astype(f32), 0.0)
     upstream_all = jnp.concatenate(group_gather(upstream.astype(bf16)), axis=0)
 
-    columns_of = output_places(relatives, seq_vector, second_parts)
+    columns_of = output_places(relatives, seq_vector, first_parts)
     output_blocks = [columns_of[0]] + [exchange(columns_of[j], SEQ, j) for j in range(1, GROUP)]
     input_full, queries, keys, values, attended, totals = attention_forward(
         relatives, normed_all, first_parts, second_parts, query_bias_part, value_bias_part, all_segments

time: 373 us -> 373 us (level)
  transfers between devices with their start and end apart: 87 -> 87, of which waited for: 23 -> 22; matrix products, arithmetic and copies ran while one was open for 9% -> 9% of each run, Pallas kernels for 25% -> 25%
where the time goes in v2:
time: 373 us; the launch traced here: 370 us
  starting transfers between devices  120 us (32%)
  Pallas kernels  110 us (29%)
  waiting for transfers between devices  91.7 us (25%)
  other arithmetic  24.9 us (7%)
  local copies, waits for them, and re-layouts  19.4 us (5%)
    ppermute x87, starting transfers between devices, exchange(): return lax.ppermute(value, axis, [(i, i ^ distance) for i in range(size)])  120 us
    pallas_call x23, Pallas kernels, local_call(): pl.pallas_call(kernel, out_shape=[jax.ShapeDtypeStruct(shape, kind) for s...  104 us
    ppermute x87, waiting for transfers between devices, exchange(): return lax.ppermute(value, axis, [(i, i ^ distance) for i in range(size)])  91.7 us
    unnamed x235, local copies, waits for them, and re-layouts  11 us
  transfers between devices with their start and end apart: 87, of which 22 were waited for; matrix products, arithmetic and copies ran while one was open for 9% of the time, Pallas kernels for 25%

profile of v2, /device:TPU:1, one launch (start us, length us, event | category | flops | bytes accessed | tf_op | source)
XLA Modules:
  0.0 370.3 jit_solution(14524402399417176708)
XLA Ops:
  24.4 4.8 %collective-permute-start = (bf16[152,1024]{1,0:T(8,128)(2,1)S(1)}, bf16[152,1024]{1,0:T(8,128)(2,1)S(1)}, u32[]{:S(2)}, u32[]{:S(2)}) collective-permute-start(bf16[152,1024]{1,0:T(8,128)(2,1)S(1)} %add_convert_fusion.4), channel_id=1, source_target_pairs={{0,1},{1,0},{2,3},{3,2},{4,5},{5,4},{6,7},{7,6},{8,9},{9,8},{10,11... | collective-permute-start | bytes 933896 | tf_op jit(solution)/shard_map/ppermute | solution.py:81
  40.2 4.8 %collective-permute-start.17 = (bf16[256,256]{1,0:T(8,128)(2,1)S(1)}, bf16[256,256]{1,0:T(8,128)(2,1)S(1)}, u32[]{:S(2)}, u32[]{:S(2)}) collective-permute-start(bf16[256,256]{1,0:T(8,128)(2,1)S(1)} %get-tuple-element.163), channel_id=1, source_target_pairs={{0,1},{1,0},{2,3},{3,2},{4,5},{5,4},{6,7},{7,6},{8,9},{9,8},{10,11... | collective-permute-start | bytes 393224 | tf_op jit(solution)/shard_map/ppermute | solution.py:81
  48.7 12.4 %shard_map.298 = (bf16[1024,768]{1,0:T(8,128)(2,1)}, bf16[4,152,256]{2,1,0:T(8,128)(2,1)}, bf16[608,256]{1,0:T(8,128)(2,1)}, bf16[608,256]{1,0:T(8,128)(2,1)}, b...) custom-call(s32[8]{0:T(128)} %iota_xor_fusion.1.index_ref, bf16[608,1024]{1,0:T(8,128)(2,1)} %pad_maximum_fusion.x_ref.left_ref, ...), custom_call_target="tpu_custom_call" | custom-call | tf_op jit(solution)/shard_map/pallas_call | solution.py:206
  61.8 2.8 shard_map.300
  86.0 10.4 %collective-permute-start.32 = (bf16[152,1024]{1,0:T(8,128)(2,1)S(1)}, bf16[152,1024]{1,0:T(8,128)(2,1)S(1)}, u32[]{:S(2)}, u32[]{:S(2)}) collective-permute-start(bf16[152,1024]{1,0:T(8,128)(2,1)S(1)} %fusion.3), channel_id=1, source_target_pairs={{0,1},{1,0},{2,3},{3,2},{4,5},{5,4},{6,7},{7,6},{8,9},{9,8},{10,11... | collective-permute-start | bytes 933896 | tf_op jit(solution)/shard_map/ppermute | solution.py:81
  99.6 15.8 %collective-permute-done.38.refs_4_ = bf16[128,1024]{1,0:T(8,128)(2,1)S(1)} collective-permute-done((bf16[128,1024]{1,0:T(8,128)(2,1)S(1)}, bf16[128,1024]{1,0:T(8,128)(2,1)S(1)}, u32[]{:S(2)}, u32[]{:S(2)}) %collective-permute-start.38) | collective-permute-done | bytes 262176 | tf_op jit(solution)/shard_map/ppermute | solution.py:81
  116.5 3.9 %collective-permute-start.34 = (bf16[152,1024]{1,0:T(8,128)(2,1)S(1)}, bf16[152,1024]{1,0:T(8,128)(2,1)S(1)}, u32[]{:S(2)}, u32[]{:S(2)}) collective-permute-start(bf16[152,1024]{1,0:T(8,128)(2,1)S(1)} %collective-permute-done.33), channel_id=1, source_target_pairs={{0,1},{1,0},{2,3},{3,2},{4,5},{5,4},{6,7},{7,6},{8,9},{9,8},{10,11... | collective-permute-start | bytes 933896 | tf_op jit(solution)/shard_map/ppermute | solution.py:81
  121.9 3.8 %collective-permute-start.24 = (bf16[152,1024]{1,0:T(8,128)(2,1)S(1)}, bf16[152,1024]{1,0:T(8,128)(2,1)S(1)}, u32[]{:S(2)}, u32[]{:S(2)}) collective-permute-start(bf16[152,1024]{1,0:T(8,128)(2,1)S(1)} %collective-permute-done.23.refs_2_), channel_id=1, source_target_pairs={{0,1},{1,0},{2,3},{3,2},{4,5},{5,4},{6,7},{7,6},{8,9},{9,8},{10,11... | collective-permute-start | bytes 933896 | tf_op jit(solution)/shard_map/ppermute | solution.py:81
  129.1 4.4 %collective-permute-done.31.refs_11_ = bf16[128,1024]{1,0:T(8,128)(2,1)S(1)} collective-permute-done((bf16[128,1024]{1,0:T(8,128)(2,1)S(1)}, bf16[128,1024]{1,0:T(8,128)(2,1)S(1)}, u32[]{:S(2)}, u32[]{:S(2)}) %collective-permute-start.31) | collective-permute-done | bytes 262176 | tf_op jit(solution)/shard_map/ppermute | solution.py:81
  139.4 8.8 %shard_map.302 = (bf16[1024,1024]{1,0:T(8,128)(2,1)}, bf16[4,152,1024]{2,1,0:T(8,128)(2,1)}, bf16[4,152,1024]{2,1,0:T(8,128)(2,1)}, f32[4,152,1024]{2,1,0:T(8,128)}) custom-call(s32[8]{0:T(128)} %iota_xor_fusion.1.index_ref, bf16[152,1024]{1,0:T(8,128)(2,1)} %copy-done.8, bf16[152,1024]{1,0:T(8,128)(2,1)} %copy-done.34, bf16[152,1024]{1,0:T(8,128)(2,1)} %copy-done.33, ...), custom_call_target="tpu_custom_call" | custom-call | tf_op jit(solution)/shard_map/pallas_call | solution.py:206
  150.4 5.6 %collective-permute-done.41.refs_7_ = bf16[128,1024]{1,0:T(8,128)(2,1)S(1)} collective-permute-done((bf16[128,1024]{1,0:T(8,128)(2,1)S(1)}, bf16[128,1024]{1,0:T(8,128)(2,1)S(1)}, u32[]{:S(2)}, u32[]{:S(2)}) %collective-permute-start.41) | collective-permute-done | bytes 262176 | tf_op jit(solution)/shard_map/ppermute | solution.py:81
  156.7 10.2 %shard_map.303 = (bf16[1024,1024]{1,0:T(8,128)(2,1)}, bf16[4,152,1024]{2,1,0:T(8,128)(2,1)}, f32[1,1024]{1,0:T(1,128)}, bf16[2,152,1024]{2,1,0:T(8,128)(2,1)}, f32[2,152,1024]{2,1,0:T(8,128)}) custom-call(s32[8]{0:T(128)} %iota_xor_fusion.1.index_ref, bf16[4,152,1024]{2,1,0:T(8,128)(2,1)} %bitcast.92, bf16[128,1024]{1,0:T(8,128)(2,1)} %get-tuple-element.79.refs_0_, ...), custom_call_target="tpu_custom_call" | custom-call | tf_op jit(solution)/shard_map/pallas_call | solution.py:206
  171.5 8.3 %collective-permute-done.45 = bf16[152,1024]{1,0:T(8,128)(2,1)S(1)} collective-permute-done((bf16[152,1024]{1,0:T(8,128)(2,1)S(1)}, bf16[152,1024]{1,0:T(8,128)(2,1)S(1)}, u32[]{:S(2)}, u32[]{:S(2)}) %collective-permute-start.45) | collective-permute-done | bytes 311328 | tf_op jit(solution)/shard_map/ppermute | solution.py:81
  182.7 4.9 %shard_map.315 = (bf16[4,128,1024]{2,1,0:T(8,128)(2,1)}, f32[4,128,1024]{2,1,0:T(8,128)}) custom-call(s32[8]{0:T(128)} %iota_xor_fusion.1.index_ref, bf16[608,1024]{1,0:T(8,128)(2,1)} %bitcast.97, bf16[608,1024]{1,0:T(8,128)(2,1)} %bitcast.98), custom_call_target="tpu_custom_call" | custom-call | tf_op jit(solution)/shard_map/pallas_call | solution.py:206
  188.8 4.9 %shard_map.319 = (bf16[4,128,1024]{2,1,0:T(8,128)(2,1)}, f32[4,128,1024]{2,1,0:T(8,128)}) custom-call(s32[8]{0:T(128)} %iota_xor_fusion.1.index_ref, bf16[608,1024]{1,0:T(8,128)(2,1)} %bitcast.93, bf16[608,1024]{1,0:T(8,128)(2,1)} %pad_maximum_fusion.1.right_ref), custom_call_target="tpu_custom_call" | custom-call | tf_op jit(solution)/shard_map/pallas_call | solution.py:206
  199.0 13.5 %shard_map.307 = (bf16[608,768]{1,0:T(8,128)(2,1)}, f32[1,768]{1,0:T(1,128)}) custom-call(s32[1]{0:T(128)} %constant.196.clone.1.zero_ref, bf16[4,152,256]{2,1,0:T(8,128)(2,1)} %get-tuple-element.85.q_ref, bf16[608,256]{1,0:T(8,128)(2,1)} %get-tuple-element.86.k_ref, bf16[608,256]{1,0:T(8,128)(2,1)} %get-tuple-element.87.v_ref, ...), custom_call_target="tpu_custom_call" | custom-call | tf_op jit(solution)/shard_map/pallas_call | solution.py:206
  212.6 4.9 %shard_map.308 = (bf16[2,152,1024]{2,1,0:T(8,128)(2,1)}, f32[2,152,1024]{2,1,0:T(8,128)}) custom-call(s32[1]{0:T(128)} %constant.196.clone.1.zero_ref, bf16[4,152,768]{2,1,0:T(8,128)(2,1)} %bitcast.94, bf16[1024,768]{1,0:T(8,128)(2,1)} %get-tuple-element.93.right_ref), custom_call_target="tpu_custom_call" | custom-call | tf_op jit(solution)/shard_map/pallas_call | solution.py:206
  217.9 4.6 %shard_map.304 = (bf16[2,152,1024]{2,1,0:T(8,128)(2,1)}, f32[2,152,1024]{2,1,0:T(8,128)}) custom-call(s32[1]{0:T(128)} %constant.196.clone.1.zero_ref, bf16[4,152,1024]{2,1,0:T(8,128)(2,1)} %get-tuple-element.78.left_ref, bf16[1024,1024]{1,0:T(8,128)(2,1)} %get-tuple-element.82.right_ref), custom_call_target="tpu_custom_call" | custom-call | tf_op jit(solution)/shard_map/pallas_call | solution.py:206
  224.0 3.0 shard_map.316
  227.0 3.7 %collective-permute-start.74 = (bf16[128,1024]{1,0:T(8,128)(2,1)}, bf16[128,1024]{1,0:T(8,128)(2,1)}, u32[]{:S(2)}, u32[]{:S(2)}) collective-permute-start(bf16[128,1024]{1,0:T(8,128)(2,1)} %get-tuple-element.119), channel_id=1, source_target_pairs={{0,8},{4,12},{8,0},{12,4},{16,24},{20,28},{24,16},{28,20},{1,9},{5... | collective-permute-start | bytes 786440 | tf_op jit(solution)/shard_map/ppermute | solution.py:81
  230.7 3.0 collective-permute-done.80.received_ref
  234.6 3.0 shard_map.320
  237.7 4.3 %shard_map.309 = (bf16[4,128,768]{2,1,0:T(8,128)(2,1)}, f32[4,128,768]{2,1,0:T(8,128)}) custom-call(s32[8]{0:T(128)} %iota_xor_fusion.1.index_ref, bf16[608,1024]{1,0:T(8,128)(2,1)} %pad_maximum_fusion.x_ref.left_ref, bf16[608,768]{1,0:T(8,128)(2,1)} %get-tuple-element.92.right_ref), custom_call_target="tpu_custom_call" | custom-call | tf_op jit(solution)/shard_map/pallas_call | solution.py:206
  245.6 2.7 shard_map.311
  257.0 4.8 %collective-permute-start.75 = (bf16[128,1024]{1,0:T(8,128)(2,1)}, bf16[128,1024]{1,0:T(8,128)(2,1)S(1)}, u32[]{:S(2)}, u32[]{:S(2)}) collective-permute-start(bf16[128,1024]{1,0:T(8,128)(2,1)} %get-tuple-element.120), channel_id=1, source_target_pairs={{0,16},{4,20},{8,24},{12,28},{16,0},{20,4},{24,8},{28,12},{1,17},{... | collective-permute-start | bytes 786440 | tf_op jit(solution)/shard_map/ppermute | solution.py:81
  267.0 12.9 %collective-permute-done.75.refs_2_ = bf16[128,1024]{1,0:T(8,128)(2,1)S(1)} collective-permute-done((bf16[128,1024]{1,0:T(8,128)(2,1)}, bf16[128,1024]{1,0:T(8,128)(2,1)S(1)}, u32[]{:S(2)}, u32[]{:S(2)}) %collective-permute-start.75) | collective-permute-done | bytes 262176 | tf_op jit(solution)/shard_map/ppermute | solution.py:81
  287.1 15.3 %collective-permute-done.82.refs_2_ = bf16[128,1024]{1,0:T(8,128)(2,1)S(1)} collective-permute-done((bf16[128,1024]{1,0:T(8,128)(2,1)}, bf16[128,1024]{1,0:T(8,128)(2,1)S(1)}, u32[]{:S(2)}, u32[]{:S(2)}) %collective-permute-start.82) | collective-permute-done | bytes 262176 | tf_op jit(solution)/shard_map/ppermute | solution.py:81
  310.6 5.1 %collective-permute-start.67 = (bf16[128,256]{1,0:T(8,128)(2,1)}, bf16[128,256]{1,0:T(8,128)(2,1)S(1)}, u32[]{:S(2)}, u32[]{:S(2)}) collective-permute-start(bf16[128,256]{1,0:T(8,128)(2,1)} %get-tuple-element.109), channel_id=1, source_target_pairs={{0,8},{4,12},{8,0},{12,4},{16,24},{20,28},{24,16},{28,20},{1,9},{5... | collective-permute-start | bytes 196616 | tf_op jit(solution)/shard_map/ppermute | solution.py:81
  318.2 3.7 collective-permute-done.85.refs_2_
  334.6 7.6 %collective-permute-done.60.refs_1_ = bf16[128,768]{1,0:T(8,128)(2,1)S(1)} collective-permute-done((bf16[128,768]{1,0:T(8,128)(2,1)}, bf16[128,768]{1,0:T(8,128)(2,1)S(1)}, u32[]{:S(2)}, u32[]{:S(2)}) %collective-permute-start.60) | collective-permute-done | bytes 196640 | tf_op jit(solution)/shard_map/ppermute | solution.py:81
  342.8 5.8 %collective-permute-start.79 = (bf16[128,1024]{1,0:T(8,128)(2,1)S(1)}, bf16[128,1024]{1,0:T(8,128)(2,1)S(1)}, u32[]{:S(2)}, u32[]{:S(2)}) collective-permute-start(bf16[128,1024]{1,0:T(8,128)(2,1)S(1)} %collective-permute-done.78.refs_2_), channel_id=1, source_target_pairs={{0,1},{1,0},{2,3},{3,2},{4,5},{5,4},{6,7},{7,6},{8,9},{9,8},{10,11... | collective-permute-start | bytes 786440 | tf_op jit(solution)/shard_map/ppermute | solution.py:81
  356.8 2.8 shard_map.318
  (483 shorter events, 161.7 us)
Async XLA Ops:
  2.4 17.7 %collective-permute-start.3 = (bf16[128,512]{1,0:T(8,128)(2,1)}, bf16[128,512]{1,0:T(8,128)(2,1)S(1)}, u32[]{:S(2)}, u32[]{:S(2)}) collective-permute-start(bf16[128,512]{1,0:T(8,128)(2,1)} %get-tuple-element.72.refs_0_), channel_id=1, source_target_pairs={{0,4},{4,0},{8,12},{12,8},{16,20},{20,16},{24,28},{28,24},{1,5},{5... | collective-permute-start | bytes 393224 | tf_op jit(solution)/shard_map/ppermute | solution.py:81
  24.4 20.7 %collective-permute-start = (bf16[152,1024]{1,0:T(8,128)(2,1)S(1)}, bf16[152,1024]{1,0:T(8,128)(2,1)S(1)}, u32[]{:S(2)}, u32[]{:S(2)}) collective-permute-start(bf16[152,1024]{1,0:T(8,128)(2,1)S(1)} %add_convert_fusion.4), channel_id=1, source_target_pairs={{0,1},{1,0},{2,3},{3,2},{4,5},{5,4},{6,7},{7,6},{8,9},{9,8},{10,11... | collective-permute-start | bytes 933896 | tf_op jit(solution)/shard_map/ppermute | solution.py:81
  29.1 16.2 %collective-permute-start.2 = (bf16[152,1024]{1,0:T(8,128)(2,1)S(1)}, bf16[152,1024]{1,0:T(8,128)(2,1)S(1)}, u32[]{:S(2)}, u32[]{:S(2)}) collective-permute-start(bf16[152,1024]{1,0:T(8,128)(2,1)S(1)} %collective-permute-done.1), channel_id=1, source_target_pairs={{0,1},{1,0},{2,3},{3,2},{4,5},{5,4},{6,7},{7,6},{8,9},{9,8},{10,11... | collective-permute-start | bytes 933896 | tf_op jit(solution)/shard_map/ppermute | solution.py:81
  40.2 20.9 %collective-permute-start.17 = (bf16[256,256]{1,0:T(8,128)(2,1)S(1)}, bf16[256,256]{1,0:T(8,128)(2,1)S(1)}, u32[]{:S(2)}, u32[]{:S(2)}) collective-permute-start(bf16[256,256]{1,0:T(8,128)(2,1)S(1)} %get-tuple-element.163), channel_id=1, source_target_pairs={{0,1},{1,0},{2,3},{3,2},{4,5},{5,4},{6,7},{7,6},{8,9},{9,8},{10,11... | collective-permute-start | bytes 393224 | tf_op jit(solution)/shard_map/ppermute | solution.py:81
  75.4 21.0 %collective-permute-start.30 = (bf16[128,1024]{1,0:T(8,128)(2,1)}, bf16[128,1024]{1,0:T(8,128)(2,1)S(1)}, u32[]{:S(2)}, u32[]{:S(2)}) collective-permute-start(bf16[128,1024]{1,0:T(8,128)(2,1)} %get-tuple-element.77.refs_4_), channel_id=1, source_target_pairs={{0,24},{4,28},{8,16},{12,20},{16,8},{20,12},{24,0},{28,4},{1,25},{... | collective-permute-start | bytes 786440 | tf_op jit(solution)/shard_map/ppermute | solution.py:81
  78.1 20.5 %collective-permute-start.36 = (bf16[128,1024]{1,0:T(8,128)(2,1)}, bf16[128,1024]{1,0:T(8,128)(2,1)S(1)}, u32[]{:S(2)}, u32[]{:S(2)}) collective-permute-start(bf16[128,1024]{1,0:T(8,128)(2,1)} %get-tuple-element.79.refs_0_), channel_id=1, source_target_pairs={{0,8},{4,12},{8,0},{12,4},{16,24},{20,28},{24,16},{28,20},{1,9},{5... | collective-permute-start | bytes 786440 | tf_op jit(solution)/shard_map/ppermute | solution.py:81
  81.3 34.1 %collective-permute-start.38 = (bf16[128,1024]{1,0:T(8,128)(2,1)S(1)}, bf16[128,1024]{1,0:T(8,128)(2,1)S(1)}, u32[]{:S(2)}, u32[]{:S(2)}) collective-permute-start(bf16[128,1024]{1,0:T(8,128)(2,1)S(1)} %copy-done.36), channel_id=1, source_target_pairs={{0,16},{4,20},{8,24},{12,28},{16,0},{20,4},{24,8},{28,12},{1,17},{... | collective-permute-start | bytes 786440 | tf_op jit(solution)/shard_map/ppermute | solution.py:81
  84.9 31.5 %collective-permute-start.33 = (bf16[152,1024]{1,0:T(8,128)(2,1)S(1)}, bf16[152,1024]{1,0:T(8,128)(2,1)S(1)}, u32[]{:S(2)}, u32[]{:S(2)}) collective-permute-start(bf16[152,1024]{1,0:T(8,128)(2,1)S(1)} %fusion.3), channel_id=1, source_target_pairs={{0,2},{1,3},{2,0},{3,1},{4,6},{5,7},{6,4},{7,5},{8,10},{9,11},{10,... | collective-permute-start | bytes 933896 | tf_op jit(solution)/shard_map/ppermute | solution.py:81
  86.0 34.5 %collective-permute-start.32 = (bf16[152,1024]{1,0:T(8,128)(2,1)S(1)}, bf16[152,1024]{1,0:T(8,128)(2,1)S(1)}, u32[]{:S(2)}, u32[]{:S(2)}) collective-permute-start(bf16[152,1024]{1,0:T(8,128)(2,1)S(1)} %fusion.3), channel_id=1, source_target_pairs={{0,1},{1,0},{2,3},{3,2},{4,5},{5,4},{6,7},{7,6},{8,9},{9,8},{10,11... | collective-permute-start | bytes 933896 | tf_op jit(solution)/shard_map/ppermute | solution.py:81
  96.4 24.0 %collective-permute-start.40 = (bf16[128,1024]{1,0:T(8,128)(2,1)S(1)}, bf16[128,1024]{1,0:T(8,128)(2,1)S(1)}, u32[]{:S(2)}, u32[]{:S(2)}) collective-permute-start(bf16[128,1024]{1,0:T(8,128)(2,1)S(1)} %copy-done.36), channel_id=1, source_target_pairs={{0,24},{4,28},{8,16},{12,20},{16,8},{20,12},{24,0},{28,4},{1,25},{... | collective-permute-start | bytes 786440 | tf_op jit(solution)/shard_map/ppermute | solution.py:81
  98.6 23.0 %collective-permute-start.27 = (bf16[128,1024]{1,0:T(8,128)(2,1)S(1)}, bf16[128,1024]{1,0:T(8,128)(2,1)S(1)}, u32[]{:S(2)}, u32[]{:S(2)}) collective-permute-start(bf16[128,1024]{1,0:T(8,128)(2,1)S(1)} %collective-permute-done.26.refs_6_), channel_id=1, source_target_pairs={{0,4},{4,0},{8,12},{12,8},{16,20},{20,16},{24,28},{28,24},{1,5},{5... | collective-permute-start | bytes 786440 | tf_op jit(solution)/shard_map/ppermute | solution.py:81
  116.5 18.3 %collective-permute-start.34 = (bf16[152,1024]{1,0:T(8,128)(2,1)S(1)}, bf16[152,1024]{1,0:T(8,128)(2,1)S(1)}, u32[]{:S(2)}, u32[]{:S(2)}) collective-permute-start(bf16[152,1024]{1,0:T(8,128)(2,1)S(1)} %collective-permute-done.33), channel_id=1, source_target_pairs={{0,1},{1,0},{2,3},{3,2},{4,5},{5,4},{6,7},{7,6},{8,9},{9,8},{10,11... | collective-permute-start | bytes 933896 | tf_op jit(solution)/shard_map/ppermute | solution.py:81
  121.9 16.7 %collective-permute-start.24 = (bf16[152,1024]{1,0:T(8,128)(2,1)S(1)}, bf16[152,1024]{1,0:T(8,128)(2,1)S(1)}, u32[]{:S(2)}, u32[]{:S(2)}) collective-permute-start(bf16[152,1024]{1,0:T(8,128)(2,1)S(1)} %collective-permute-done.23.refs_2_), channel_id=1, source_target_pairs={{0,1},{1,0},{2,3},{3,2},{4,5},{5,4},{6,7},{7,6},{8,9},{9,8},{10,11... | collective-permute-start | bytes 933896 | tf_op jit(solution)/shard_map/ppermute | solution.py:81
  127.9 20.4 %collective-permute-start.35 = (bf16[128,1024]{1,0:T(8,128)(2,1)S(1)}, bf16[128,1024]{1,0:T(8,128)(2,1)S(1)}, u32[]{:S(2)}, u32[]{:S(2)}) collective-permute-start(bf16[128,1024]{1,0:T(8,128)(2,1)S(1)} %copy-done.36), channel_id=1, source_target_pairs={{0,4},{4,0},{8,12},{12,8},{16,20},{20,16},{24,28},{28,24},{1,5},{5... | collective-permute-start | bytes 786440 | tf_op jit(solution)/shard_map/ppermute | solution.py:81
  135.0 21.0 %collective-permute-start.41 = (bf16[128,1024]{1,0:T(8,128)(2,1)S(1)}, bf16[128,1024]{1,0:T(8,128)(2,1)S(1)}, u32[]{:S(2)}, u32[]{:S(2)}) collective-permute-start(bf16[128,1024]{1,0:T(8,128)(2,1)S(1)} %collective-permute-done.40.refs_6_), channel_id=1, source_target_pairs={{0,4},{4,0},{8,12},{12,8},{16,20},{20,16},{24,28},{28,24},{1,5},{5... | collective-permute-start | bytes 786440 | tf_op jit(solution)/shard_map/ppermute | solution.py:81
  187.6 36.4 %collective-permute-start.73 = (bf16[4,128,1024]{2,1,0:T(8,128)(2,1)}, bf16[4,128,1024]{2,1,0:T(8,128)(2,1)}, u32[]{:S(2)}, u32[]{:S(2)}) collective-permute-start(bf16[4,128,1024]{2,1,0:T(8,128)(2,1)} %get-tuple-element.117), channel_id=1, source_target_pairs={{0,4},{4,0},{8,12},{12,8},{16,20},{20,16},{24,28},{28,24},{1,5},{5... | collective-permute-start | bytes 3145736 | tf_op jit(solution)/shard_map/ppermute | solution.py:81
  193.8 39.9 %collective-permute-start.80 = (bf16[4,128,1024]{2,1,0:T(8,128)(2,1)}, bf16[4,128,1024]{2,1,0:T(8,128)(2,1)S(1)}, u32[]{:S(2)}, u32[]{:S(2)}) collective-permute-start(bf16[4,128,1024]{2,1,0:T(8,128)(2,1)} %get-tuple-element.123), channel_id=1, source_target_pairs={{0,4},{4,0},{8,12},{12,8},{16,20},{20,16},{24,28},{28,24},{1,5},{5... | collective-permute-start | bytes 3145736 | tf_op jit(solution)/shard_map/ppermute | solution.py:81
  217.5 24.5 %collective-permute-start.49 = (bf16[2,152,1024]{2,1,0:T(8,128)(2,1)}, bf16[2,152,1024]{2,1,0:T(8,128)(2,1)}, u32[]{:S(2)}, u32[]{:S(2)}) collective-permute-start(bf16[2,152,1024]{2,1,0:T(8,128)(2,1)} %get-tuple-element.95), channel_id=1, source_target_pairs={{0,1},{1,0},{2,3},{3,2},{4,5},{5,4},{6,7},{7,6},{8,9},{9,8},{10,11... | collective-permute-start | bytes 1867784 | tf_op jit(solution)/shard_map/ppermute | solution.py:81
  222.4 41.2 %collective-permute-start.42 = (bf16[2,152,1024]{2,1,0:T(8,128)(2,1)}, bf16[2,152,1024]{2,1,0:T(8,128)(2,1)S(1)}, u32[]{:S(2)}, u32[]{:S(2)}) collective-permute-start(bf16[2,152,1024]{2,1,0:T(8,128)(2,1)} %get-tuple-element.84), channel_id=1, source_target_pairs={{0,1},{1,0},{2,3},{3,2},{4,5},{5,4},{6,7},{7,6},{8,9},{9,8},{10,11... | collective-permute-start | bytes 1867784 | tf_op jit(solution)/shard_map/ppermute | solution.py:81
  227.0 38.7 %collective-permute-start.74 = (bf16[128,1024]{1,0:T(8,128)(2,1)}, bf16[128,1024]{1,0:T(8,128)(2,1)}, u32[]{:S(2)}, u32[]{:S(2)}) collective-permute-start(bf16[128,1024]{1,0:T(8,128)(2,1)} %get-tuple-element.119), channel_id=1, source_target_pairs={{0,8},{4,12},{8,0},{12,4},{16,24},{20,28},{24,16},{28,20},{1,9},{5... | collective-permute-start | bytes 786440 | tf_op jit(solution)/shard_map/ppermute | solution.py:81
  257.0 22.9 %collective-permute-start.75 = (bf16[128,1024]{1,0:T(8,128)(2,1)}, bf16[128,1024]{1,0:T(8,128)(2,1)S(1)}, u32[]{:S(2)}, u32[]{:S(2)}) collective-permute-start(bf16[128,1024]{1,0:T(8,128)(2,1)} %get-tuple-element.120), channel_id=1, source_target_pairs={{0,16},{4,20},{8,24},{12,28},{16,0},{20,4},{24,8},{28,12},{1,17},{... | collective-permute-start | bytes 786440 | tf_op jit(solution)/shard_map/ppermute | solution.py:81
  261.8 19.2 %collective-permute-start.76 = (bf16[128,1024]{1,0:T(8,128)(2,1)}, bf16[128,1024]{1,0:T(8,128)(2,1)S(1)}, u32[]{:S(2)}, u32[]{:S(2)}) collective-permute-start(bf16[128,1024]{1,0:T(8,128)(2,1)} %get-tuple-element.121), channel_id=1, source_target_pairs={{0,24},{4,28},{8,16},{12,20},{16,8},{20,12},{24,0},{28,4},{1,25},{... | collective-permute-start | bytes 786440 | tf_op jit(solution)/shard_map/ppermute | solution.py:81
  263.7 18.0 %collective-permute-start.81 = (bf16[128,1024]{1,0:T(8,128)(2,1)S(1)}, bf16[128,1024]{1,0:T(8,128)(2,1)S(1)}, u32[]{:S(2)}, u32[]{:S(2)}) collective-permute-start(bf16[128,1024]{1,0:T(8,128)(2,1)S(1)} %copy-done.113), channel_id=1, source_target_pairs={{0,8},{4,12},{8,0},{12,4},{16,24},{20,28},{24,16},{28,20},{1,9},{5... | collective-permute-start | bytes 786440 | tf_op jit(solution)/shard_map/ppermute | solution.py:81
  264.5 58.4 %collective-permute-start.59 = (bf16[4,128,768]{2,1,0:T(8,128)(2,1)}, bf16[4,128,768]{2,1,0:T(8,128)(2,1)S(1)}, u32[]{:S(2)}, u32[]{:S(2)}) collective-permute-start(bf16[4,128,768]{2,1,0:T(8,128)(2,1)} %get-tuple-element.99), channel_id=1, source_target_pairs={{0,4},{4,0},{8,12},{12,8},{16,20},{20,16},{24,28},{28,24},{1,5},{5... | collective-permute-start | bytes 2359304 | tf_op jit(solution)/shard_map/ppermute | solution.py:81
  265.7 36.7 %collective-permute-start.82 = (bf16[128,1024]{1,0:T(8,128)(2,1)}, bf16[128,1024]{1,0:T(8,128)(2,1)S(1)}, u32[]{:S(2)}, u32[]{:S(2)}) collective-permute-start(bf16[128,1024]{1,0:T(8,128)(2,1)} %get-tuple-element.126), channel_id=1, source_target_pairs={{0,16},{4,20},{8,24},{12,28},{16,0},{20,4},{24,8},{28,12},{1,17},{... | collective-permute-start | bytes 786440 | tf_op jit(solution)/shard_map/ppermute | solution.py:81
  280.0 22.8 %collective-permute-start.83 = (bf16[128,1024]{1,0:T(8,128)(2,1)}, bf16[128,1024]{1,0:T(8,128)(2,1)}, u32[]{:S(2)}, u32[]{:S(2)}) collective-permute-start(bf16[128,1024]{1,0:T(8,128)(2,1)} %get-tuple-element.127), channel_id=1, source_target_pairs={{0,24},{4,28},{8,16},{12,20},{16,8},{20,12},{24,0},{28,4},{1,25},{... | collective-permute-start | bytes 786440 | tf_op jit(solution)/shard_map/ppermute | solution.py:81
  281.1 24.9 %collective-permute-start.52 = (f32[16,1024]{1,0:T(8,128)S(1)}, f32[16,1024]{1,0:T(8,128)S(1)}, u32[]{:S(2)}, u32[]{:S(2)}) collective-permute-start(f32[16,1024]{1,0:T(8,128)S(1)} %dynamic-slice_bitcast_fusion.1), channel_id=1, source_target_pairs={{0,2},{1,3},{2,0},{3,1},{4,6},{5,7},{6,4},{7,5},{8,10},{9,11},{10,... | collective-permute-start | bytes 196616 | tf_op jit(solution)/shard_map/ppermute | solution.py:81
  281.6 24.7 %collective-permute-start.66 = (bf16[4,128,256]{2,1,0:T(8,128)(2,1)S(1)}, bf16[4,128,256]{2,1,0:T(8,128)(2,1)S(1)}, u32[]{:S(2)}, u32[]{:S(2)}) collective-permute-start(bf16[4,128,256]{2,1,0:T(8,128)(2,1)S(1)} %pad_maximum_fusion.4), channel_id=1, source_target_pairs={{0,4},{4,0},{8,12},{12,8},{16,20},{20,16},{24,28},{28,24},{1,5},{5... | collective-permute-start | bytes 786440 | tf_op jit(solution)/shard_map/ppermute | solution.py:81
  326.4 25.3 %collective-permute-start.77 = (bf16[128,1024]{1,0:T(8,128)(2,1)S(1)}, bf16[128,1024]{1,0:T(8,128)(2,1)S(1)}, u32[]{:S(2)}, u32[]{:S(2)}) collective-permute-start(bf16[128,1024]{1,0:T(8,128)(2,1)S(1)} %copy-done.11), channel_id=1, source_target_pairs={{0,1},{1,0},{2,3},{3,2},{4,5},{5,4},{6,7},{7,6},{8,9},{9,8},{10,11... | collective-permute-start | bytes 786440 | tf_op jit(solution)/shard_map/ppermute | solution.py:81
  332.0 16.5 %collective-permute-start.62 = (bf16[128,768]{1,0:T(8,128)(2,1)}, bf16[128,768]{1,0:T(8,128)(2,1)S(1)}, u32[]{:S(2)}, u32[]{:S(2)}) collective-permute-start(bf16[128,768]{1,0:T(8,128)(2,1)} %get-tuple-element.103), channel_id=1, source_target_pairs={{0,24},{4,28},{8,16},{12,20},{16,8},{20,12},{24,0},{28,4},{1,25},{... | collective-permute-start | bytes 589832 | tf_op jit(solution)/shard_map/ppermute | solution.py:81
  334.2 17.1 %collective-permute-start.57 = (f32[16,1024]{1,0:T(8,128)S(1)}, f32[16,1024]{1,0:T(8,128)S(1)}, u32[]{:S(2)}, u32[]{:S(2)}) collective-permute-start(f32[16,1024]{1,0:T(8,128)S(1)} %add_add_fusion.4), channel_id=1, source_target_pairs={{0,2},{1,3},{2,0},{3,1},{4,6},{5,7},{6,4},{7,5},{8,10},{9,11},{10,... | collective-permute-start | bytes 196616 | tf_op jit(solution)/shard_map/ppermute | solution.py:81
  342.2 17.4 %collective-permute-start.84 = (bf16[128,1024]{1,0:T(8,128)(2,1)S(1)}, bf16[128,1024]{1,0:T(8,128)(2,1)S(1)}, u32[]{:S(2)}, u32[]{:S(2)}) collective-permute-start(bf16[128,1024]{1,0:T(8,128)(2,1)S(1)} %copy-done.12), channel_id=1, source_target_pairs={{0,1},{1,0},{2,3},{3,2},{4,5},{5,4},{6,7},{7,6},{8,9},{9,8},{10,11... | collective-permute-start | bytes 786440 | tf_op jit(solution)/shard_map/ppermute | solution.py:81
  (170 other events, 1863.4 us)
